TPU v7x, 32 devices: a whole 2x2x4 slice. The times are simulated.
32 devices in a mesh: dom: 8 (over z, y), grp: 4 (over x, core).
Axes of the slice: x: 2, y: 2, z: 4, core: 2. Of those that a mesh axis runs over, the one named last changes fastest.
Arguments:
- old_state: float32 [9, 56, 4096], P(None, None, ('dom', 'grp')), may hold values from -6 to 6
- stiffness: float32 [3, 56, 56], replicated, may hold values from -0.75 to 0.75
- jacobians: float32 [3, 9, 9, 4096], P(None, None, None, ('dom', 'grp')), may hold values from -2 to 2
- lift_own: float32 [4, 56, 56], replicated, may hold values from -0.75 to 0.75
- lift_across: float32 [4, 4, 56, 56], replicated, may hold values from -0.75 to 0.75
- riemann: float32 [2, 4, 9, 9, 4096], P(None, None, None, None, ('dom', 'grp')), may hold values from -2 to 2
- cluster_ids: int32 [4096], P(('dom', 'grp')), may hold values from 0 to 2
- send_slots: int32 [10240], P(('dom', 'grp')), may hold values from 0 to 127, as said below
- face_partner: int32 [4, 4096], P(None, ('dom', 'grp')), may hold values from 0 to 447, as said below
- partner_face: int32 [4, 4096], P(None, ('dom', 'grp')), may hold values from 0 to 3
- cohesion: float32 [4096], P(('dom', 'grp')), may hold values from 1 to 4
- relax_time: float32 [4096], P(('dom', 'grp')), may hold values from 0.1 to 1
- yield_flag: int32 [4096], P(('dom', 'grp')), may hold values 0 or 1
Outputs:
- new_state: float32 [9, 56, 4096], P(None, None, ('dom', 'grp'))
Inputs may be any that keep to these rules, and one draw needn't show every extreme that they name: `send_slots`: local element numbers of the sending device; its first 256 slots go in equal shares to the devices of its grp group in grp order, the next 32 to the device one index lower along dom and the last 32 to the one one index higher, cyclically; the slots bound for one destination name distinct elements. `face_partner`: a place of the device's neighbour list: own elements, then what the grp group sends it, sender by sender, then what the lower and the higher dom neighbour send it; every received place is the partner of exactly one face of the device, all other faces have own places.
All inputs are finite; a program needn't handle non-finite values. No bound on the sum of `yield_flag` on one device may be relied on, other than what follows from the above.
Results may differ from a plain program's by a relative error of at most 0.0003.
Values sent between devices are 32-bit elements; how exact they have to be, the bound alone decides.
No kernel may reach another device: no remote copies, remote signals or barrier semaphores. Data moves between devices by JAX's collectives and lax.ppermute only.
A program may use at most 64 MiB of HBM per device.

v0:
```python
import jax
import jax.numpy as jnp
from jax import lax
from jax.sharding import PartitionSpec as P

QUANT = 9
MODES = 56
ORDER = 6
GRP_SLOTS = 256
HALO = 32


base_step = 0.2
highest = lax.Precision.HIGHEST


def with_halo(shard, sides, width):
    for axis, dim in sides:
        count, length = (lax.axis_size(axis), shard.shape[dim])
        up = [(i, (i + 1) % count) for i in range(count)]
        down = [(j, i) for i, j in up]
        last = lax.slice_in_dim(shard, length - width, length, axis=dim)
        initial = lax.slice_in_dim(shard, 0, width, axis=dim)
        before = lax.ppermute(last, axis, up)
        after = lax.ppermute(initial, axis, down)
        shard = jnp.concatenate([before, shard, after], axis=dim)
    return shard


def step_table(terms_count):
    entries = []
    for rate_level in range(3):
        interval = base_step * 2.0**rate_level
        factorial = 1.0
        powers = []
        for degree in range(terms_count):
            factorial = factorial * (degree + 1)
            powers.append(interval ** (degree + 1) / factorial)
        entries.append(powers)
    return jnp.array(entries, dtype=jnp.float32)


def clock_steps():
    return jnp.array([base_step, 2.0 * base_step, 4.0 * base_step], dtype=jnp.float32)


def cluster_selector(cluster_ids):
    return (cluster_ids[None, :] == jnp.arange(3, dtype=jnp.int32)[:, None]).astype(jnp.float32)


def on_modes(matrix, operand):
    return jnp.einsum("mn,qne->qme", matrix, operand, precision=highest)


def on_quantities(operand, blocks):
    return jnp.sum(operand[:, None, :, :] * blocks[:, :, None, :], axis=0)


def taylor_stack(initial, stiffness, jacobian):
    collected = [initial]
    for degree in range(1, ORDER):
        latest = collected[-1]
        change = on_quantities(on_modes(stiffness[0], latest), jacobian[0])
        change = change + on_quantities(on_modes(stiffness[1], latest), jacobian[1])
        change = change + on_quantities(on_modes(stiffness[2], latest), jacobian[2])
        collected.append(-change)
    return jnp.stack(collected)


def integrate(stacked, weights):
    summed = weights[0] * stacked[0]
    for degree in range(1, stacked.shape[0]):
        summed = summed + weights[degree] * stacked[degree]
    return summed


def all_levels(collected, taylor_table):
    return jnp.stack(
        [integrate(collected, taylor_table[rate_level][:, None]) for rate_level in range(3)]
    )


def volume_term(own_int, stiffness, jacobian):
    summed = on_modes(stiffness[0].T, on_quantities(own_int, jacobian[0]))
    summed = summed + on_modes(stiffness[1].T, on_quantities(own_int, jacobian[1]))
    summed = summed + on_modes(stiffness[2].T, on_quantities(own_int, jacobian[2]))
    return summed


def face_update(own_int, neighbours, partner_sides, lift_own, lift_across, riemann):
    summed = jnp.zeros_like(own_int)
    candidates = jnp.arange(4, dtype=jnp.int32)[:, None]
    for face_index in range(4):
        summed = summed + on_quantities(
            on_modes(lift_own[face_index], own_int), riemann[0, face_index]
        )
        projected = jnp.einsum(
            "jmn,qne->qjme", lift_across[face_index], neighbours[face_index], precision=highest
        )
        picker = (partner_sides[face_index][None, :] == candidates).astype(jnp.float32)
        chosen = jnp.sum(projected * picker[None, :, None, :], axis=1)
        summed = summed + on_quantities(chosen, riemann[1, face_index])
    return summed


def plastic(updated, cohesion, relax_time, yielding, interval):
    isotropic = (jnp.arange(6, dtype=jnp.int32) < 3).astype(jnp.float32)[:, None, None]
    pressure = (updated[0] + updated[1] + updated[2]) / 3.0
    deviator = updated[:6] - isotropic * pressure[None]
    centre = deviator[:, 0, :]
    second = 0.5 * (centre[0] * centre[0] + centre[1] * centre[1] + centre[2] * centre[2])
    second = second + centre[3] * centre[3] + centre[4] * centre[4] + centre[5] * centre[5]
    strength = jnp.sqrt(second)
    excess = jnp.maximum(strength - cohesion, 0.0) / jnp.maximum(strength, cohesion)
    factor = yielding.astype(jnp.float32) * excess * (1.0 - jnp.exp(-interval / relax_time))
    return jnp.concatenate([updated[:6] - factor[None, None, :] * deviator, updated[6:]], axis=0)


def advance(
    own_block,
    stiffness,
    jacobian,
    lift_own,
    lift_across,
    riemann,
    selector,
    own_int,
    neighbours,
    partner_sides,
    cohesion,
    relax_time,
    yielding,
):
    updated = own_block + volume_term(own_int, stiffness, jacobian)
    updated = updated - face_update(
        own_int, neighbours, partner_sides, lift_own, lift_across, riemann
    )
    interval = jnp.sum(selector * clock_steps()[:, None], axis=0)
    return plastic(updated, cohesion, relax_time, yielding, interval)


def on_device(
    old_state,
    stiffness,
    jacobians,
    lift_own,
    lift_across,
    riemann,
    cluster_ids,
    send_slots,
    face_partner,
    partner_face,
    cohesion,
    relax_time,
    yield_flag,
):
    owned = old_state.shape[2]
    taylor_table = step_table(ORDER)
    selector = cluster_selector(cluster_ids)
    own_weights = jnp.sum(selector[:, None, :] * taylor_table[:, :, None], axis=0)
    collected = taylor_stack(old_state, stiffness, jacobians)
    own_int = integrate(collected, own_weights)
    payload = all_levels(collected, taylor_table).reshape(-1, owned)
    outgoing = jnp.take(payload, send_slots, axis=1)
    from_peers = lax.all_to_all(
        outgoing[:, :GRP_SLOTS], "grp", split_axis=1, concat_axis=1, tiled=True
    )
    padded = with_halo(outgoing[:, GRP_SLOTS:], (("dom", 1),), HALO)
    remote = jnp.concatenate([from_peers, padded[:, :HALO], padded[:, -HALO:]], axis=1)
    listing = jnp.concatenate([payload, remote], axis=1)
    neighbours = []
    for face_index in range(4):
        picked = jnp.take(listing, face_partner[face_index], axis=1)
        picked = picked.reshape(3, QUANT, MODES, owned)
        neighbours.append(jnp.sum(picked * selector[:, None, None, :], axis=0))
    return advance(
        old_state,
        stiffness,
        jacobians,
        lift_own,
        lift_across,
        riemann,
        selector,
        own_int,
        neighbours,
        partner_face,
        cohesion,
        relax_time,
        yield_flag,
    )


def solution(mesh):
    in_specs = (
        P(None, None, ("dom", "grp")),
        P(),
        P(None, None, None, ("dom", "grp")),
        P(),
        P(),
        P(None, None, None, None, ("dom", "grp")),
        P(("dom", "grp")),
        P(("dom", "grp")),
        P(None, ("dom", "grp")),
        P(None, ("dom", "grp")),
        P(("dom", "grp")),
        P(("dom", "grp")),
        P(("dom", "grp")),
    )
    out_specs = P(None, None, ("dom", "grp"))
    return jax.shard_map(
        on_device, mesh=mesh, in_specs=in_specs, out_specs=out_specs, check_vma=False
    )
```

profile of v0, /device:TPU:0, one launch (start us, length us, event | category | flops | bytes accessed | tf_op | source)
XLA Modules:
  0.0 73.9 jit_solution(13080536704117318930)
XLA Ops:
  0.0 1.3 %convolution_bitcast_fusion.20 = f32[9,56,128]{2,1,0:T(8,128)S(1)} fusion(f32[9,56,128]{2,1,0:T(8,128)} %param.17, f32[3,56,56]{2,1,0:T(8,128)} %param.18), kind=kOutput, calls=%fused_computation.66 | convolution fusion | flops 43352064 | bytes 544768 | tf_op jit(solution)/shard_map/mn,qne->qme/dot_general | solution.py:52
  1.4 1.4 %convolution_bitcast_fusion.21 = f32[9,56,128]{2,1,0:T(8,128)S(1)} fusion(f32[9,56,128]{2,1,0:T(8,128)} %param.17, f32[3,56,56]{2,1,0:T(8,128)} %param.18), kind=kOutput, calls=%fused_computation.67 | convolution fusion | flops 43352064 | bytes 544768 | tf_op jit(solution)/shard_map/mn,qne->qme/dot_general | solution.py:52
  2.8 1.4 %convolution_bitcast_fusion.22 = f32[9,56,128]{2,1,0:T(8,128)S(1)} fusion(f32[9,56,128]{2,1,0:T(8,128)} %param.17, f32[3,56,56]{2,1,0:T(8,128)} %param.18), kind=kOutput, calls=%fused_computation.68 | convolution fusion | flops 43352064 | bytes 544768 | tf_op jit(solution)/shard_map/mn,qne->qme/dot_general | solution.py:52
  4.1 1.2 %fusion.85 = (f32[1,9,9,128]{3,0,2,1:T(1,128)S(1)}, f32[1,9,9,128]{3,0,2,1:T(1,128)S(1)}, f32[1,9,9,128]{3,0,2,1:T(1,128)S(1)}) fusion(f32[3,9,9,128]{3,0,2,1:T(4,128)} %param.19), kind=kLoop, calls=%fused_computation.220 | loop fusion | bytes 248832 | tf_op jit(solution)/shard_map/slice | solution.py:64
  5.9 0.4 convolution_bitcast_fusion.18
  6.3 0.4 convolution_bitcast_fusion.17
  6.7 0.4 convolution_bitcast_fusion.19
  7.7 0.4 convolution_bitcast_fusion.15
  8.1 0.4 convolution_bitcast_fusion.14
  8.5 0.4 convolution_bitcast_fusion.16
  9.5 0.4 convolution_bitcast_fusion.12
  9.9 0.4 convolution_bitcast_fusion.13
  10.3 0.4 convolution_bitcast_fusion.11
  11.7 0.4 convolution_bitcast_fusion.10
  12.1 0.4 convolution_bitcast_fusion.8
  14.0 2.0 %gather_fusion = f32[320,1512]{1,0:T(8,128)S(1)} fusion(f32[1512,128]{0,1:T(8,128)S(1)} %copy.49, s32[1024]{0:T(1024)S(1)} %pad_clamp_fusion.4), kind=kCustom, calls=%fused_computation.4 | custom fusion | bytes 3872000 | tf_op jit(solution)/shard_map/jit(_take)/gather | solution.py:164
  16.2 1.3 %copy-done.2 = f32[1512,320]{0,1:T(8,128)} copy-done((f32[1512,320]{0,1:T(8,128)}, f32[1512,320]{0,1:T(8,128)S(1)}, u32[]{:S(2)}) %copy-start.2) | copy-done | bytes 1935384
  17.5 1.3 %slice.374 = f32[1512,256]{0,1:T(8,128)} slice(f32[1512,320]{0,1:T(8,128)S(1)} %select_bitcast_fusion), slice={[0:1512], [0:256]} | slice | bytes 3096576 | tf_op jit(solution)/shard_map/slice | solution.py:166
  18.8 4.4 %all-to-all-start = ((f32[1512,4,64]{0,2,1:T(8,128)}), f32[1512,4,64]{0,2,1:T(8,128)S(1)}, u32[]{:S(2)}, u32[]{:S(2)}) async-start(f32[1512,4,64]{0,2,1:T(8,128)} %bitcast.44), calls=%async_computation | async-start | bytes 3145728 | tf_op jit(solution)/shard_map/all_to_all | solution.py:165
  23.2 1.1 %fusion.83 = (f32[1512,32]{0,1:T(8,128)S(1)}, f32[1512,32]{0,1:T(8,128)S(1)}) fusion(f32[1512,320]{0,1:T(8,128)} %copy-done.2), kind=kLoop, calls=%fused_computation.218 | loop fusion | bytes 774144 | tf_op jit(solution)/shard_map/slice | solution.py:22
  24.3 2.4 %collective-permute-start = (f32[1512,32]{0,1:T(8,128)S(1)}, f32[1512,32]{0,1:T(8,128)S(1)}, u32[]{:S(2)}, u32[]{:S(2)}) collective-permute-start(f32[1512,32]{0,1:T(8,128)S(1)} %get-tuple-element.23), channel_id=1, source_target_pairs={{0,4},{4,8},{8,12},{12,16},{16,20},{20,24},{24,28},{28,0},{1,5},{5... | collective-permute-start | bytes 580616 | tf_op jit(solution)/shard_map/ppermute | solution.py:24
  26.7 3.3 %collective-permute-start.1 = (f32[1512,32]{0,1:T(8,128)S(1)}, f32[1512,32]{0,1:T(8,128)}, u32[]{:S(2)}, u32[]{:S(2)}) collective-permute-start(f32[1512,32]{0,1:T(8,128)S(1)} %get-tuple-element.24), channel_id=1, source_target_pairs={{4,0},{8,4},{12,8},{16,12},{20,16},{24,20},{28,24},{0,28},{5,1},{9... | collective-permute-start | bytes 580616 | tf_op jit(solution)/shard_map/ppermute | solution.py:25
  30.4 0.4 convolution_bitcast_fusion.5
  30.8 0.4 convolution_bitcast_fusion.6
  31.2 0.4 convolution_bitcast_fusion.7
  31.6 1.3 %multiply_reduce_fusion.8 = (f32[9,56,128]{2,1,0:T(8,128)}, f32[9,56,128]{2,1,0:T(8,128)S(1)}, f32[9,56,128]{2,1,0:T(8,128)S(1)}) fusion(f32[9,56,128]{2,1,0:T(8,128)S(1)} %get-tuple-element.27, f32[9,9,128]{2,1,0:T(8,128)S(1)} %get-tuple-element.55, f32[9,9,128]{2,1,0:T(8,128)S(1)} %get-tuple-element.56, f32[9,9,128]{2,1,0:T(8,128)S(1)} %bitcast.289), kind=kLoop, calls=%fused_computation.14 | loop fusion | flops 3290112 | bytes 1156608 | tf_op jit(solution)/shard_map/reduce_sum | solution.py:56
  32.8 0.6 compare_and_fusion
  33.7 0.7 select_reduce_fusion
  34.3 0.6 pad_clamp_fusion.2
  34.9 0.6 pad_clamp_fusion
  35.5 0.6 copy_bitcast_fusion.2
  36.2 0.6 copy_bitcast_fusion.4
  36.8 0.6 copy_bitcast_fusion.6
  37.4 0.6 copy_bitcast_fusion
  38.1 0.9 %multiply_reduce_fusion.1 = f32[9,56,128]{2,1,0:T(8,128)} fusion(f32[9,9,128]{2,1,0:T(8,128)S(1)} %get-tuple-element.58, f32[9,56,128]{2,1,0:T(8,128)S(1)} %convolution_bitcast_fusion.4), kind=kLoop, calls=%fused_computation.7 | loop fusion | flops 1096704 | bytes 557568 | tf_op jit(solution)/shard_map/reduce_sum | solution.py:56
  38.9 0.9 %multiply_reduce_fusion.3 = f32[9,56,128]{2,1,0:T(8,128)} fusion(f32[9,9,128]{2,1,0:T(8,128)S(1)} %get-tuple-element.60, f32[9,56,128]{2,1,0:T(8,128)S(1)} %convolution_bitcast_fusion.5), kind=kLoop, calls=%fused_computation.9 | loop fusion | flops 1096704 | bytes 557568 | tf_op jit(solution)/shard_map/reduce_sum | solution.py:56
  39.8 0.9 %multiply_reduce_fusion.5 = f32[9,56,128]{2,1,0:T(8,128)} fusion(f32[9,9,128]{2,1,0:T(8,128)S(1)} %get-tuple-element.62, f32[9,56,128]{2,1,0:T(8,128)S(1)} %convolution_bitcast_fusion.6), kind=kLoop, calls=%fused_computation.11 | loop fusion | flops 1096704 | bytes 557568 | tf_op jit(solution)/shard_map/reduce_sum | solution.py:56
  40.6 0.9 %multiply_reduce_fusion.7 = f32[9,56,128]{2,1,0:T(8,128)} fusion(f32[9,9,128]{2,1,0:T(8,128)S(1)} %get-tuple-element.64, f32[9,56,128]{2,1,0:T(8,128)S(1)} %convolution_bitcast_fusion.7), kind=kLoop, calls=%fused_computation.13 | loop fusion | flops 1096704 | bytes 557568 | tf_op jit(solution)/shard_map/reduce_sum | solution.py:56
  41.5 0.5 compare_convert_fusion
  42.0 0.4 fusion.41
  42.5 1.2 %convolution_add_fusion.1 = f32[9,128,56]{1,2,0:T(8,128)} fusion(f32[9,128,56]{1,2,0:T(8,128)S(1)} %fusion.41, f32[9,56,128]{2,1,0:T(8,128)S(1)} %get-tuple-element.7, f32[3,56,56]{2,1,0:T(8,128)S(1)} %copy-done.7), kind=kOutput, calls=%fused_computation.49 | convolution fusion | flops 43416576 | bytes 802816 | tf_op jit(solution)/shard_map/mn,qne->qme/dot_general | solution.py:52
  43.6 0.6 fusion.71
  44.2 0.7 copy-done.20
  44.9 1.1 %copy-done.3 = f32[1512,4,64]{0,2,1:T(8,128)} copy-done((f32[1512,4,64]{0,2,1:T(8,128)}, f32[1512,4,64]{0,2,1:T(8,128)S(1)}, u32[]{:S(2)}) %copy-start.3) | copy-done | bytes 1548312
  46.0 1.8 %pad_maximum_fusion = f32[1512,448]{0,1:T(8,128)S(1)} fusion(f32[1512,32]{0,1:T(8,128)} %collective-permute-done.1, f32[1512,32]{0,1:T(8,128)} %copy-done.20, f32[1512,256]{0,1:T(8,128)} %bitcast.283, f32[1512,128]{0,1:T(8,128)S(1)} %copy.49), kind=kLoop, calls=%fused_computation.5 | loop fusion | flops 2032128 | bytes 5419008 | tf_op jit(solution)/shard_map/concatenate | solution.py:170
  47.8 1.9 %gather_fusion.2 = f32[128,1512]{1,0:T(8,128)} fusion(f32[1512,448]{0,1:T(8,128)S(1)} %pad_maximum_fusion, s32[1024]{0:T(1024)} %get-tuple-element.71), kind=kCustom, calls=%fused_computation.1.clone | custom fusion | bytes 1548800 | tf_op jit(solution)/shard_map/jit(_take)/gather | solution.py:173
  49.7 1.3 %select_bitcast_fusion.3 = f32[1512,128]{0,1:T(8,128)S(1)} fusion(f32[128,1512]{1,0:T(8,128)} %gather_fusion.2, pred[128]{0:T(512)(128)(4,1)} %get-tuple-element.49), kind=kLoop, calls=%fused_computation.71 | loop fusion | flops 193536 | bytes 1548416 | tf_op jit(solution)/shard_map/jit(_take)/select_n | solution.py:173
  51.0 1.1 %copy.53 = f32[1512,128]{1,0:T(8,128)} copy(f32[1512,128]{0,1:T(8,128)S(1)} %select_bitcast_fusion.3) | data formatting | bytes 1548288 | tf_op jit(solution)/shard_map/jit(_take)/select_n | solution.py:173
  52.1 1.9 %gather_fusion.3 = f32[128,1512]{1,0:T(8,128)} fusion(f32[1512,448]{0,1:T(8,128)S(1)} %pad_maximum_fusion, s32[1024]{0:T(1024)} %get-tuple-element.70), kind=kCustom, calls=%fused_computation.2.clone | custom fusion | bytes 1548800 | tf_op jit(solution)/shard_map/jit(_take)/gather | solution.py:173
  54.0 1.3 %select_bitcast_fusion.2 = f32[1512,128]{0,1:T(8,128)S(1)} fusion(f32[128,1512]{1,0:T(8,128)} %gather_fusion.3, pred[128]{0:T(512)(128)(4,1)} %get-tuple-element.53), kind=kLoop, calls=%fused_computation.70 | loop fusion | flops 193536 | bytes 1548416 | tf_op jit(solution)/shard_map/jit(_take)/select_n | solution.py:173
  55.2 1.2 %copy.56 = f32[1512,128]{1,0:T(8,128)} copy(f32[1512,128]{0,1:T(8,128)S(1)} %select_bitcast_fusion.2) | data formatting | bytes 1548288 | tf_op jit(solution)/shard_map/jit(_take)/select_n | solution.py:173
  56.4 1.9 %gather_fusion.4 = f32[128,1512]{1,0:T(8,128)} fusion(f32[1512,448]{0,1:T(8,128)S(1)} %pad_maximum_fusion, s32[1024]{0:T(1024)} %get-tuple-element.69), kind=kCustom, calls=%fused_computation.3.clone | custom fusion | bytes 1548800 | tf_op jit(solution)/shard_map/jit(_take)/gather | solution.py:173
  58.3 1.3 %select_bitcast_fusion.1 = f32[1512,128]{0,1:T(8,128)S(1)} fusion(f32[128,1512]{1,0:T(8,128)} %gather_fusion.4, pred[128]{0:T(512)(128)(4,1)} %get-tuple-element.13), kind=kLoop, calls=%fused_computation.69 | loop fusion | flops 193536 | bytes 1548416 | tf_op jit(solution)/shard_map/jit(_take)/select_n | solution.py:173
  59.5 1.2 %copy.59 = f32[1512,128]{1,0:T(8,128)} copy(f32[1512,128]{0,1:T(8,128)S(1)} %select_bitcast_fusion.1) | data formatting | bytes 1548288 | tf_op jit(solution)/shard_map/jit(_take)/select_n | solution.py:173
  60.7 1.9 %gather_fusion.1 = f32[128,1512]{1,0:T(8,128)} fusion(f32[1512,448]{0,1:T(8,128)S(1)} %pad_maximum_fusion, s32[1024]{0:T(1024)} %get-tuple-element.72), kind=kCustom, calls=%fused_computation.clone | custom fusion | bytes 1548800 | tf_op jit(solution)/shard_map/jit(_take)/gather | solution.py:173
  62.5 1.4 %select_bitcast_fusion.4 = f32[1512,128]{0,1:T(8,128)S(1)} fusion(f32[128,1512]{1,0:T(8,128)} %gather_fusion.1, pred[128]{0:T(512)(128)(4,1)} %get-tuple-element.51), kind=kLoop, calls=%fused_computation.72 | loop fusion | flops 193536 | bytes 1548416 | tf_op jit(solution)/shard_map/jit(_take)/select_n | solution.py:173
  64.0 1.1 %copy.50 = f32[1512,128]{1,0:T(8,128)} copy(f32[1512,128]{0,1:T(8,128)S(1)} %select_bitcast_fusion.4) | data formatting | bytes 1548288 | tf_op jit(solution)/shard_map/jit(_take)/select_n | solution.py:173
  65.1 1.6 %multiply_reduce_fusion.29 = (f32[9,56,128]{2,1,0:T(8,128)S(1)}, f32[9,56,128]{2,1,0:T(8,128)S(1)}, f32[9,56,128]{2,1,0:T(8,128)S(1)}, f32[9,56,128]{2,1,0:T(8,128)S(1)}) fusion(f32[3,9,56,128]{3,2,1,0:T(8,128)} %bitcast.293, f32[3,128]{1,0:T(4,128)S(1)} %fusion.70, f32[3,9,56,128]{3,2,1,0:T(8,128)S(1)} %bitcast.290, f32[3,9,56,128]{3,2,1,0:T(8,128)S(1)} %bitcast.291, ...), kind=kLoop, calls=%fused_computation.77 | loop fusion | flops 1290240 | bytes 4130304 | tf_op jit(solution)/shard_map/reduce_sum | solution.py:175
  66.9 1.0 %fusion.5 = f32[9,56,128]{2,1,0:T(8,128)S(1)} fusion(f32[4,128]{1,0:T(4,128)S(1)} %get-tuple-element.67, f32[9,56,128]{2,1,0:T(8,128)S(1)} %get-tuple-element.11, f32[4,4,56,56]{3,2,1,0:T(8,128)S(1)} %copy-done.14), kind=kOutput, calls=%fused_computation.42 | convolution fusion | flops 173859840 | bytes 632832 | tf_op jit(solution)/shard_map/jmn,qne->qjme/dot_general | solution.py:97
  68.0 1.0 %fusion.6 = f32[9,56,128]{2,1,0:T(8,128)S(1)} fusion(f32[4,128]{1,0:T(4,128)S(1)} %copy-done.22, f32[9,56,128]{2,1,0:T(8,128)S(1)} %get-tuple-element.10, f32[4,4,56,56]{3,2,1,0:T(8,128)S(1)} %copy-done.14), kind=kOutput, calls=%fused_computation.43 | convolution fusion | flops 173859840 | bytes 632832 | tf_op jit(solution)/shard_map/jmn,qne->qjme/dot_general | solution.py:97
  69.2 1.0 %fusion.7 = f32[9,56,128]{2,1,0:T(8,128)S(1)} fusion(f32[4,128]{1,0:T(4,128)S(1)} %get-tuple-element.65, f32[9,56,128]{2,1,0:T(8,128)S(1)} %get-tuple-element.9, f32[4,4,56,56]{3,2,1,0:T(8,128)S(1)} %copy-done.14), kind=kOutput, calls=%fused_computation.44 | convolution fusion | flops 173859840 | bytes 632832 | tf_op jit(solution)/shard_map/jmn,qne->qjme/dot_general | solution.py:97
  70.3 1.0 %fusion.4 = f32[9,56,128]{2,1,0:T(8,128)S(1)} fusion(f32[4,128]{1,0:T(4,128)S(1)} %get-tuple-element.68, f32[9,56,128]{2,1,0:T(8,128)S(1)} %get-tuple-element.12, f32[4,4,56,56]{3,2,1,0:T(8,128)S(1)} %copy-done.14), kind=kOutput, calls=%fused_computation.41 | convolution fusion | flops 173859840 | bytes 632832 | tf_op jit(solution)/shard_map/jmn,qne->qjme/dot_general | solution.py:97
  71.6 1.3 %fusion.10 = f32[9,56,128]{2,1,0:T(8,128)S(1)} fusion(f32[9,56,128]{2,1,0:T(8,128)S(1)} %copy-done.1, f32[9,128,56]{1,2,0:T(8,128)S(1)} %copy-done.13, f32[9,56,128]{2,1,0:T(8,128)S(1)} %copy-done.8, f32[9,56,128]{2,1,0:T(8,128)S(1)} %multiply_reduce_fusion, f32[9,56,128]{2,1,0:T(8,128)S(1)} %copy-done.9, f32[9,56,128]{2,1,0:T(8,128)S(1)} %multiply_reduce_fusion.2, ...), kind=kOutput, calls=%fused_computation.48 | convolution fusion | flops 43997184 | bytes 3125248 | tf_op jit(solution)/shard_map/mn,qne->qme/dot_general | solution.py:52
  73.2 0.7 pad_maximum_fusion.2
  (114 shorter events, 6.0 us)
Async XLA Ops:
  1.4 4.6 %copy-start.7 = (f32[3,56,56]{2,1,0:T(8,128)S(1)}, f32[3,56,56]{2,1,0:T(8,128)}, u32[]{:S(2)}) copy-start(f32[3,56,56]{2,1,0:T(8,128)} %param.18) | copy-start | bytes 112900
  10.7 1.8 %copy-start.23 = (s32[320]{0:T(512)S(1)}, s32[320]{0:T(512)}, u32[]{:S(2)}) copy-start(s32[320]{0:T(512)} %param.24) | copy-start | bytes 3844
  11.2 1.8 %copy-start.28 = (s32[128]{0:T(128)S(1)}, s32[128]{0:T(128)}, u32[]{:S(2)}) copy-start(s32[128]{0:T(128)} %param.23) | copy-start | bytes 1540
  11.2 1.9 %copy-start.27 = (f32[3,6]{1,0:T(4,128)S(1)}, f32[3,6]{1,0:T(4,128)}, u32[]{:S(2)}) copy-start(f32[3,6]{1,0:T(4,128)} %constant.43.clone) | copy-start | bytes 220
  11.2 1.9 %copy-start = (f32[9,56,128]{2,1,0:T(8,128)S(1)}, f32[9,56,128]{2,1,0:T(8,128)}, u32[]{:S(2)}) copy-start(f32[9,56,128]{2,1,0:T(8,128)} %param.17) | copy-start | bytes 774148
  16.2 1.3 %copy-start.2 = (f32[1512,320]{0,1:T(8,128)}, f32[1512,320]{0,1:T(8,128)S(1)}, u32[]{:S(2)}) copy-start(f32[1512,320]{0,1:T(8,128)S(1)} %select_bitcast_fusion) | copy-start | bytes 5806084
  18.8 11.2 %copy-start.21 = (f32[4,56,56]{2,1,0:T(8,128)S(1)}, f32[4,56,56]{2,1,0:T(8,128)}, u32[]{:S(2)}) copy-start(f32[4,56,56]{2,1,0:T(8,128)} %param.20) | copy-start | bytes 150532
  18.8 26.1 %all-to-all-start = ((f32[1512,4,64]{0,2,1:T(8,128)}), f32[1512,4,64]{0,2,1:T(8,128)S(1)}, u32[]{:S(2)}, u32[]{:S(2)}) async-start(f32[1512,4,64]{0,2,1:T(8,128)} %bitcast.44), calls=%async_computation | async-start | bytes 3145728 | tf_op jit(solution)/shard_map/all_to_all | solution.py:165
  23.2 9.7 %copy-start.25 = (s32[4,128]{1,0:T(4,128)S(1)}, s32[4,128]{1,0:T(4,128)}, u32[]{:S(2)}) copy-start(s32[4,128]{1,0:T(4,128)} %param.25) | copy-start | bytes 6148
  23.2 10.3 %copy-start.15 = (f32[2,4,9,9,128]{4,1,3,2,0:T(4,128)S(1)}, f32[2,4,9,9,128]{4,1,3,2,0:T(4,128)}, u32[]{:S(2)}) copy-start(f32[2,4,9,9,128]{4,1,3,2,0:T(4,128)} %param.22) | copy-start | bytes 995332
  23.2 10.5 %copy-start.33 = (f32[3]{0:T(128)S(1)}, f32[3]{0:T(128)}, u32[]{:S(2)}) copy-start(f32[3]{0:T(128)} %constant.44.clone) | copy-start | bytes 40
  24.3 19.9 %collective-permute-start = (f32[1512,32]{0,1:T(8,128)S(1)}, f32[1512,32]{0,1:T(8,128)S(1)}, u32[]{:S(2)}, u32[]{:S(2)}) collective-permute-start(f32[1512,32]{0,1:T(8,128)S(1)} %get-tuple-element.23), channel_id=1, source_target_pairs={{0,4},{4,8},{8,12},{12,16},{16,20},{20,24},{24,28},{28,0},{1,5},{5... | collective-permute-start | bytes 580616 | tf_op jit(solution)/shard_map/ppermute | solution.py:24
  26.7 18.2 %collective-permute-start.1 = (f32[1512,32]{0,1:T(8,128)S(1)}, f32[1512,32]{0,1:T(8,128)}, u32[]{:S(2)}, u32[]{:S(2)}) collective-permute-start(f32[1512,32]{0,1:T(8,128)S(1)} %get-tuple-element.24), channel_id=1, source_target_pairs={{4,0},{8,4},{12,8},{16,12},{20,16},{24,20},{28,24},{0,28},{5,1},{9... | collective-permute-start | bytes 580616 | tf_op jit(solution)/shard_map/ppermute | solution.py:25
  31.6 10.5 %copy-start.26 = (s32[4,128]{1,0:T(4,128)S(1)}, s32[4,128]{1,0:T(4,128)}, u32[]{:S(2)}) copy-start(s32[4,128]{1,0:T(4,128)} %param.26) | copy-start | bytes 6148
  44.2 0.7 copy-start.20
  44.9 1.1 %copy-start.3 = (f32[1512,4,64]{0,2,1:T(8,128)}, f32[1512,4,64]{0,2,1:T(8,128)S(1)}, u32[]{:S(2)}) copy-start(f32[1512,4,64]{0,2,1:T(8,128)S(1)} %all-to-all-done) | copy-start | bytes 4644868
  62.5 2.6 %copy-start.4 = (f32[1512,128]{1,0:T(8,128)S(1)}, f32[1512,128]{1,0:T(8,128)}, u32[]{:S(2)}) copy-start(f32[1512,128]{1,0:T(8,128)} %copy.53) | copy-start | bytes 2322436
  62.5 2.6 %copy-start.5 = (f32[1512,128]{1,0:T(8,128)S(1)}, f32[1512,128]{1,0:T(8,128)}, u32[]{:S(2)}) copy-start(f32[1512,128]{1,0:T(8,128)} %copy.56) | copy-start | bytes 2322436
  62.5 2.6 %copy-start.6 = (f32[1512,128]{1,0:T(8,128)S(1)}, f32[1512,128]{1,0:T(8,128)}, u32[]{:S(2)}) copy-start(f32[1512,128]{1,0:T(8,128)} %copy.59) | copy-start | bytes 2322436
  65.1 1.7 %copy-start.14 = (f32[4,4,56,56]{3,2,1,0:T(8,128)S(1)}, f32[4,4,56,56]{3,2,1,0:T(8,128)}, u32[]{:S(2)}) copy-start(f32[4,4,56,56]{3,2,1,0:T(8,128)} %param.21) | copy-start | bytes 602116
  65.1 2.7 %copy-start.19 = (f32[9,9,128]{2,1,0:T(8,128)S(1)}, f32[9,9,128]{2,1,0:T(8,128)}, u32[]{:S(2)}) copy-start(f32[9,9,128]{2,1,0:T(8,128)} %get-tuple-element.59) | copy-start | bytes 124420
  65.1 2.9 %copy-start.22 = (f32[4,128]{1,0:T(4,128)S(1)}, f32[4,128]{1,0:T(4,128)}, u32[]{:S(2)}) copy-start(f32[4,128]{1,0:T(4,128)} %get-tuple-element.66) | copy-start | bytes 6148
  65.1 3.9 %copy-start.18 = (f32[9,9,128]{2,1,0:T(8,128)S(1)}, f32[9,9,128]{2,1,0:T(8,128)}, u32[]{:S(2)}) copy-start(f32[9,9,128]{2,1,0:T(8,128)} %get-tuple-element.61) | copy-start | bytes 124420
  66.7 3.4 %copy-start.17 = (f32[9,9,128]{2,1,0:T(8,128)S(1)}, f32[9,9,128]{2,1,0:T(8,128)}, u32[]{:S(2)}) copy-start(f32[9,9,128]{2,1,0:T(8,128)} %get-tuple-element.63) | copy-start | bytes 124420
  66.8 4.6 %copy-start.16 = (f32[9,9,128]{2,1,0:T(8,128)S(1)}, f32[9,9,128]{2,1,0:T(8,128)}, u32[]{:S(2)}) copy-start(f32[9,9,128]{2,1,0:T(8,128)} %get-tuple-element.57) | copy-start | bytes 124420
  66.8 4.7 %copy-start.1 = (f32[9,56,128]{2,1,0:T(8,128)S(1)}, f32[9,56,128]{2,1,0:T(8,128)}, u32[]{:S(2)}) copy-start(f32[9,56,128]{2,1,0:T(8,128)} %param.17) | copy-start | bytes 774148
  66.8 4.7 %copy-start.8 = (f32[9,56,128]{2,1,0:T(8,128)S(1)}, f32[9,56,128]{2,1,0:T(8,128)}, u32[]{:S(2)}) copy-start(f32[9,56,128]{2,1,0:T(8,128)} %get-tuple-element.6) | copy-start | bytes 774148
  66.8 4.7 %copy-start.9 = (f32[9,56,128]{2,1,0:T(8,128)S(1)}, f32[9,56,128]{2,1,0:T(8,128)}, u32[]{:S(2)}) copy-start(f32[9,56,128]{2,1,0:T(8,128)} %multiply_reduce_fusion.1) | copy-start | bytes 774148
  66.8 4.7 %copy-start.10 = (f32[9,56,128]{2,1,0:T(8,128)S(1)}, f32[9,56,128]{2,1,0:T(8,128)}, u32[]{:S(2)}) copy-start(f32[9,56,128]{2,1,0:T(8,128)} %multiply_reduce_fusion.3) | copy-start | bytes 774148
  66.8 4.7 %copy-start.11 = (f32[9,56,128]{2,1,0:T(8,128)S(1)}, f32[9,56,128]{2,1,0:T(8,128)}, u32[]{:S(2)}) copy-start(f32[9,56,128]{2,1,0:T(8,128)} %multiply_reduce_fusion.5) | copy-start | bytes 774148
  66.8 4.7 %copy-start.12 = (f32[9,56,128]{2,1,0:T(8,128)S(1)}, f32[9,56,128]{2,1,0:T(8,128)}, u32[]{:S(2)}) copy-start(f32[9,56,128]{2,1,0:T(8,128)} %multiply_reduce_fusion.7) | copy-start | bytes 774148
  66.8 4.7 %copy-start.13 = (f32[9,128,56]{1,2,0:T(8,128)S(1)}, f32[9,128,56]{1,2,0:T(8,128)}, u32[]{:S(2)}) copy-start(f32[9,128,56]{1,2,0:T(8,128)} %convolution_add_fusion.1) | copy-start | bytes 774148
  70.3 2.6 %copy-start.24 = (f32[6]{0:T(128)S(1)}, f32[6]{0:T(128)}, u32[]{:S(2)}) copy-start(f32[6]{0:T(128)} %compare_convert_fusion) | copy-start | bytes 76
  71.3 1.7 %copy-start.29 = (f32[128]{0:T(128)S(1)}, f32[128]{0:T(128)}, u32[]{:S(2)}) copy-start(f32[128]{0:T(128)} %param.28) | copy-start | bytes 1540
  71.3 1.7 %copy-start.30 = (f32[128]{0:T(128)S(1)}, f32[128]{0:T(128)}, u32[]{:S(2)}) copy-start(f32[128]{0:T(128)} %param.27) | copy-start | bytes 1540
  71.3 1.7 %copy-start.31 = (s32[128]{0:T(128)S(1)}, s32[128]{0:T(128)}, u32[]{:S(2)}) copy-start(s32[128]{0:T(128)} %param.29) | copy-start | bytes 1540
  71.3 1.7 %copy-start.32 = (f32[128]{0:T(128)S(1)}, f32[128]{0:T(128)}, u32[]{:S(2)}) copy-start(f32[128]{0:T(128)} %select_reduce_fusion) | copy-start | bytes 1540
where the time goes:
time: 74.4 us; the launch traced here: 73.9 us
  local copies, waits for them, and re-layouts  24 us (32%)
  other arithmetic  22 us (30%)
  matrix products  17 us (23%)
  starting transfers between devices  10.1 us (14%)
  between operations  0.82 us (1%)
    dot_general x22, matrix products, on_modes(): return jnp.einsum('mn,qne->qme', matrix, operand, precision=highest)  13.2 us
    reduce_sum x24, other arithmetic, on_quantities(): return jnp.sum(operand[:, None, :, :] * blocks[:, :, None, :], axis=0)  7.92 us
    gather x4, local copies, waits for them, and re-layouts, on_device(): picked = jnp.take(listing, face_partner[face_index], axis=1)  7.46 us
    select_n x4, other arithmetic, on_device(): picked = jnp.take(listing, face_partner[face_index], axis=1)  5.15 us
    select_n x4, local copies, waits for them, and re-layouts, on_device(): picked = jnp.take(listing, face_partner[face_index], axis=1)  4.6 us
    all_to_all x1, starting transfers between devices, on_device(): lax.all_to_all(outgoing[:, :GRP_SLOTS], 'grp', split_axis=1, concat_axis=...  4.37 us
    dot_general x4, matrix products, face_update(): jnp.einsum('jmn,qne->qjme', lift_across[face_index], neighbours[face_inde...  3.83 us
    ppermute x1, starting transfers between devices, with_halo(): after = lax.ppermute(initial, axis, down)  3.29 us
  transfers between devices with their start and end apart: 3, of which 0 were waited for; matrix products, arithmetic and copies ran while one was open for 21% of the time, Pallas kernels for 0%

commit v1 on v0

v1 whole, which is shorter than its diff:
```python
import jax
import jax.numpy as jnp
from jax import lax
from jax.experimental import pallas as pl
from jax.experimental.pallas import tpu as pltpu
from jax.sharding import PartitionSpec as P

QUANT = 9
MODES = 56
ORDER = 6
GRP_SLOTS = 256
HALO = 32
LEVELS = 3
LANES = 128
SUB = 8
ROWS = QUANT * MODES

base_step = 0.2
f32 = jnp.float32
bf16 = jnp.bfloat16
VMEM_LIMIT = 24 << 20


def round_up(value, unit):
    return -(-value // unit) * unit


def rows_per_group(total, width):
    return round_up(-(-total // (LANES // width)), SUB)


LEVEL_ROWS = round_up(LEVELS * ROWS, 4 * SUB)


def pack3_rows():
    return rows_per_group(LEVELS * ROWS, HALO)


def take(block, idx):
    return jnp.take_along_axis(
        block, jnp.broadcast_to(idx, block.shape), axis=1, mode="promise_in_bounds"
    )


def pick(ref, position):
    lane = jnp.bitwise_and(position, LANES - 1)
    tile = jnp.right_shift(position, 7)
    out = take(ref[:, 0:LANES], lane)
    for v in range(1, ref.shape[1] // LANES):
        out = jnp.where(tile == v, take(ref[:, v * LANES : (v + 1) * LANES], lane), out)
    return out


def lane_ids():
    return lax.broadcasted_iota(jnp.int32, (SUB, LANES), 1)


def device_place():
    grp = lax.axis_index("grp")
    odd = jnp.bitwise_and(lax.axis_index("dom"), 1)
    return grp, odd


def bases(n_grp):
    grp, odd = device_place()
    width = GRP_SLOTS // n_grp
    found = [(jnp.bitwise_xor(grp, k) * width, width) for k in range(1, n_grp)]
    found.append((GRP_SLOTS + HALO * (1 - odd), HALO))
    found.append((GRP_SLOTS + HALO * odd, HALO))
    return found


def split(x):
    high = x.astype(bf16).astype(f32)
    return high, x - high


def stationary(x):
    high, low = split(x)
    return jnp.concatenate([high, low, high], axis=0).astype(bf16)


def streamed(w):
    high, low = split(w)
    return jnp.concatenate([high, high, low], axis=1).astype(bf16)


def matmul(w, x):
    return jnp.dot(w, x, preferred_element_type=f32)


def row8(ref, index, sub):
    return jnp.broadcast_to(ref[(*index, pl.ds(sub, 1), slice(None))], (SUB, LANES))


def tiles(x):
    return x.reshape(x.shape[0] // SUB, SUB, LANES)


def untile(x):
    return x.reshape(x.shape[0] * SUB, LANES)


def request_kernel(n_grp, partner_ref, cluster_ref, *rest):
    outs, row_ref = rest[:-1], rest[-1]
    received = GRP_SLOTS + 2 * HALO
    owned = cluster_ref.shape[1]
    place = lax.broadcasted_iota(jnp.int32, (received, LANES), 0) + owned
    cluster = cluster_ref[...].astype(f32)
    marks = jnp.zeros((received, LANES), f32)
    for f in range(4):
        marks = jnp.where(partner_ref[f : f + 1, :] == place, cluster, marks)
    rows = lax.dot_general(
        jnp.ones((SUB, LANES), bf16),
        marks.astype(bf16),
        (((1,), (1,)), ((), ())),
        preferred_element_type=f32,
    )
    row_ref[...] = jnp.zeros(row_ref.shape, jnp.int32)
    row_ref[:, :received] = rows.astype(jnp.int32)
    lane = lane_ids()
    for out, (base, width) in zip(outs, bases(n_grp)):
        out[...] = pick(row_ref, base + jnp.bitwise_and(lane, width - 1))


def predictor_kernel(state_ref, stiff_ref, jac_ref, level_ref, w_ref, rhs_ref, y0_ref, y1_ref):
    w_ref[...] = streamed(stiff_ref[...].reshape(3 * MODES, MODES))
    level_ref[pl.ds(LEVELS * ROWS, LEVEL_ROWS - LEVELS * ROWS), :] = jnp.zeros(
        (LEVEL_ROWS - LEVELS * ROWS, LANES), f32
    )

    def column(q):
        return pl.ds(q * LANES, LANES)

    def project(y_ref, first, last):
        span = pl.ds(first * LANES, (last - first) * LANES)
        y_ref[:, span] = matmul(w_ref[...], rhs_ref[:, span])

    for q in range(QUANT):
        v = state_ref[q] * base_step
        rhs_ref[:, column(q)] = stationary(v)
        for c in range(LEVELS):
            level_ref[pl.ds(c * ROWS + q * MODES, MODES), :] = v * 2.0**c
        if q % 2 == 1 or q == QUANT - 1:
            project(y0_ref, q - q % 2, q + 1)
    for degree in range(1, ORDER):
        y_ref, next_ref = (y0_ref, y1_ref) if degree % 2 == 1 else (y1_ref, y0_ref)
        factor = -base_step / (degree + 1)
        for q in range(QUANT):
            acc = None
            for p in range(QUANT):
                for d in range(3):
                    term = tiles(y_ref[d * MODES : (d + 1) * MODES, column(p)]) * row8(jac_ref, (p, q), d)
                    acc = term if acc is None else acc + term
            v = untile(acc) * factor
            for c in range(LEVELS):
                rows = pl.ds(c * ROWS + q * MODES, MODES)
                level_ref[rows, :] = level_ref[rows, :] + v * 2.0 ** (c * (degree + 1))
            if degree < ORDER - 1:
                rhs_ref[:, column(q)] = stationary(v)
                if q % 2 == 1 or q == QUANT - 1:
                    project(next_ref, q - q % 2, q + 1)


def send_kernel(n_grp, level_ref, slot_ref, *rest):
    n_req = n_grp
    reqs, outs, row_ref = rest[:n_req], rest[n_req:-1], rest[-1]
    row_ref[...] = jnp.zeros(row_ref.shape, jnp.int32)
    row_ref[:, : slot_ref.shape[1]] = jnp.broadcast_to(slot_ref[...], (SUB, slot_ref.shape[1]))
    lane = lane_ids()
    for k, (base, width) in enumerate(bases(n_grp)):
        idx = pick(row_ref, base + jnp.bitwise_and(lane, width - 1))[:1]
        group = jnp.right_shift(lane, width.bit_length() - 1)[:1]
        height = outs[k].shape[0]
        out = None
        for g in range(LANES // width):
            if k < n_req:
                want = reqs[k][0:1, :]
                rows = min(height, ROWS - g * height)
                part = take(level_ref[pl.ds(g * height, rows), :], idx)
                for c in range(1, LEVELS):
                    other = take(level_ref[pl.ds(c * ROWS + g * height, rows), :], idx)
                    part = jnp.where(want == c, other, part)
            else:
                rows = min(height, LEVEL_ROWS - g * height)
                part = take(level_ref[pl.ds(g * height, rows), :], idx)
            if rows < height:
                part = jnp.concatenate([part, jnp.zeros((height - rows, LANES), f32)], axis=0)
            out = part if out is None else jnp.where(group == g, part, out)
        outs[k][...] = out


def own_kernel(
    n_grp, level_ref, state_ref, stiff_ref, jac_ref, lift_ref, across_ref, riem_ref,
    cluster_ref, slot_ref, partner_ref, part_ref, near_ref, wa_ref,
    row_ref, w_ref, rhs_ref, y_ref,
):
    cluster = cluster_ref[...]
    for q in range(QUANT):
        own = level_ref[pl.ds(q * MODES, MODES), :]
        for c in range(1, LEVELS):
            own = jnp.where(cluster == c, level_ref[pl.ds(c * ROWS + q * MODES, MODES), :], own)
        rhs_ref[:, pl.ds(q * LANES, LANES)] = stationary(own)
    for d in range(3):
        w_ref[pl.ds(d * MODES, MODES), :] = streamed(stiff_ref[d].T)
    w_ref[pl.ds(3 * MODES, 4 * MODES), :] = streamed(lift_ref[...].reshape(4 * MODES, MODES))
    for q in range(0, QUANT, 2):
        span = pl.ds(q * LANES, min(2, QUANT - q) * LANES)
        y_ref[:, span] = matmul(w_ref[...], rhs_ref[:, span])
    for q in range(QUANT):
        acc = tiles(state_ref[q])
        for p in range(QUANT):
            for d in range(3):
                term = tiles(y_ref[pl.ds(d * MODES, MODES), pl.ds(p * LANES, LANES)])
                acc = acc + term * row8(jac_ref, (p, q), d)
            for f in range(4):
                term = tiles(y_ref[pl.ds((3 + f) * MODES, MODES), pl.ds(p * LANES, LANES)])
                acc = acc - term * row8(riem_ref, (0, p, q), f)
        part_ref[q] = untile(acc)
    row_ref[...] = jnp.zeros(row_ref.shape, jnp.int32)
    row_ref[:, : slot_ref.shape[1]] = jnp.broadcast_to(slot_ref[...], (SUB, slot_ref.shape[1]))
    owned = cluster_ref.shape[1]
    for f in range(4):
        place = jnp.broadcast_to(partner_ref[f : f + 1, :], (SUB, LANES))
        inside = place < owned
        slot = jnp.maximum(place - owned, 0)
        idx = jnp.where(inside, place, pick(row_ref, slot))[:1]
        for q in range(QUANT):
            near = take(level_ref[pl.ds(q * MODES, MODES), :], idx)
            for c in range(1, LEVELS):
                other = take(level_ref[pl.ds(c * ROWS + q * MODES, MODES), :], idx)
                near = jnp.where(cluster == c, other, near)
            near_ref[f, pl.ds(q * MODES, MODES), :] = near
        wa_ref[f] = streamed(across_ref[f].reshape(4 * MODES, MODES))


def final_kernel(n_grp, *refs):
    n_got = n_grp + 1
    gots = refs[:n_got]
    (part_ref, near_ref, wa_ref, riem_ref, cluster_ref, partner_ref, side_ref,
     cohesion_ref, relax_ref, yield_ref, out_ref, rhs_ref, z_ref, chosen_ref) = refs[n_got:]
    owned = cluster_ref.shape[1]
    cluster = cluster_ref[...]
    table = bases(n_grp)

    def unpack(got_ref, width, first, rows, idx):
        height = got_ref.shape[0]
        parts = []
        at = first
        while at < first + rows:
            g, off = at // height, at % height
            n = min(height - off, first + rows - at)
            parts.append(take(got_ref[pl.ds(off, n), :], idx + g * width))
            at += n
        return parts[0] if len(parts) == 1 else jnp.concatenate(parts, axis=0)

    for f in range(4):
        slot = partner_ref[f : f + 1, :] - owned
        plans = []
        for k, (base, width) in enumerate(table):
            rel = slot - base
            hit = jnp.logical_and(rel >= 0, rel < width)
            plans.append((gots[k], width, hit, jnp.bitwise_and(rel, width - 1)))
        for q in range(QUANT):
            near = near_ref[f, pl.ds(q * MODES, MODES), :]
            for k, (got, width, hit, idx) in enumerate(plans):
                if k < n_grp:
                    near = jnp.where(hit, unpack(got, width, q * MODES, MODES, idx), near)
                else:
                    for c in range(LEVELS):
                        mine = jnp.logical_and(hit, cluster == c)
                        near = jnp.where(
                            mine, unpack(got, width, c * ROWS + q * MODES, MODES, idx), near
                        )
            rhs_ref[:, pl.ds(q * LANES, LANES)] = stationary(near)
        side = side_ref[f : f + 1, :]
        for q in range(0, QUANT, 2):
            n = min(2, QUANT - q)
            span = pl.ds(q * LANES, n * LANES)
            z_ref[:, span] = matmul(wa_ref[f], rhs_ref[:, span])
            for p in range(q, q + n):
                cut = pl.ds(p * LANES, LANES)
                chosen = z_ref[pl.ds(0, MODES), cut]
                for j in range(1, 4):
                    chosen = jnp.where(side == j, z_ref[pl.ds(j * MODES, MODES), cut], chosen)
                chosen_ref[f, p] = chosen
    updated = []
    for q in range(QUANT):
        acc = tiles(part_ref[q])
        for f in range(4):
            for p in range(QUANT):
                acc = acc - tiles(chosen_ref[f, p]) * row8(riem_ref, (1, p, q), f)
        out_ref[q] = untile(acc)
    heads = [out_ref[q, 0:1, :] for q in range(6)]
    mean = (heads[0] + heads[1] + heads[2]) / 3.0
    dev = [heads[q] - mean if q < 3 else heads[q] for q in range(6)]
    second = 0.5 * (dev[0] * dev[0] + dev[1] * dev[1] + dev[2] * dev[2])
    second = second + dev[3] * dev[3] + dev[4] * dev[4] + dev[5] * dev[5]
    strength = jnp.sqrt(second)
    cohesion = cohesion_ref[...]
    step = jnp.where(cluster == 0, base_step, jnp.where(cluster == 1, 2.0 * base_step, 4.0 * base_step))
    excess = jnp.maximum(strength - cohesion, 0.0) / jnp.maximum(strength, cohesion)
    factor = yield_ref[...].astype(f32) * excess * (1.0 - jnp.exp(-step / relax_ref[...]))
    pressure = (out_ref[0] + out_ref[1] + out_ref[2]) / 3.0
    for q in range(6):
        now = out_ref[q]
        out_ref[q] = now - factor * (now - pressure if q < 3 else now)


def call(kernel, out_shape, scratch, *args, cost=None, name=None):
    vmem = pl.BlockSpec(memory_space=pltpu.VMEM)
    many = isinstance(out_shape, (list, tuple))
    return pl.pallas_call(
        kernel,
        out_shape=out_shape,
        in_specs=[vmem] * len(args),
        out_specs=[vmem] * len(out_shape) if many else vmem,
        scratch_shapes=scratch,
        compiler_params=pltpu.CompilerParams(vmem_limit_bytes=VMEM_LIMIT),
        cost_estimate=cost,
        name=name,
    )(*args)


def on_device(
    n_dom, n_grp, old_state, stiffness, jacobians, lift_own, lift_across, riemann,
    cluster_ids, send_slots, face_partner, partner_face, cohesion, relax_time, yield_flag,
):
    owned = old_state.shape[2]
    slots = send_slots.shape[0]
    wide = round_up(slots, LANES)
    shape = jax.ShapeDtypeStruct
    width = GRP_SLOTS // n_grp
    jac = jnp.transpose(jacobians, (1, 2, 0, 3))
    riem = jnp.transpose(riemann, (0, 2, 3, 1, 4))
    cluster = cluster_ids.reshape(1, owned)
    slot_row = send_slots.reshape(1, slots)

    pair_low = [(i, i ^ 1) for i in range(n_dom)]
    pair_high = [(i, ((i + 1) if i % 2 else (i - 1)) % n_dom) for i in range(n_dom)]
    routes = [("grp", [(i, i ^ k) for i in range(n_grp)]) for k in range(1, n_grp)]
    routes += [("dom", pair_low), ("dom", pair_high)]
    order = sorted(range(n_grp - 1), key=lambda k: (k + 1) < 2) + [n_grp - 1]

    def request_body(*refs):
        request_kernel(n_grp, *refs)

    requests = call(
        request_body,
        [shape((SUB, LANES), jnp.int32)] * n_grp,
        [pltpu.VMEM((SUB, wide), jnp.int32)],
        face_partner, cluster, name="requests",
    )
    wanted = [None] * n_grp
    for k in order:
        wanted[k] = lax.ppermute(requests[k], *routes[k])

    levels = call(
        predictor_kernel,
        shape((LEVEL_ROWS, LANES), f32),
        [
            pltpu.VMEM((3 * MODES, 3 * MODES), bf16),
            pltpu.VMEM((3 * MODES, QUANT * LANES), bf16),
            pltpu.VMEM((3 * MODES, QUANT * LANES), f32),
            pltpu.VMEM((3 * MODES, QUANT * LANES), f32),
        ],
        old_state, stiffness, jac, name="predictor",
    )

    heights = [rows_per_group(ROWS, width)] * (n_grp - 1)
    heights += [rows_per_group(ROWS, HALO), pack3_rows()]

    def send_body(*refs):
        send_kernel(n_grp, *refs)

    outgoing = call(
        send_body,
        [shape((h, LANES), f32) for h in heights],
        [pltpu.VMEM((SUB, wide), jnp.int32)],
        levels, slot_row, *wanted, name="sends",
    )
    gots = [None] * (n_grp + 1)
    for k in order + [n_grp]:
        gots[k] = lax.ppermute(outgoing[k], *routes[k])

    def own_body(*refs):
        own_kernel(n_grp, *refs)

    partial, near, across = call(
        own_body,
        [
            shape((QUANT, MODES, LANES), f32),
            shape((4, ROWS, LANES), f32),
            shape((4, 4 * MODES, 3 * MODES), bf16),
        ],
        [
            pltpu.VMEM((SUB, wide), jnp.int32),
            pltpu.VMEM((7 * MODES, 3 * MODES), bf16),
            pltpu.VMEM((3 * MODES, QUANT * LANES), bf16),
            pltpu.VMEM((7 * MODES, QUANT * LANES), f32),
        ],
        levels, old_state, stiffness, jac, lift_own, lift_across, riem, cluster, slot_row,
        face_partner,
        cost=pl.CostEstimate(flops=10**8, bytes_accessed=4 * 10**6, transcendentals=0),
        name="own",
    )

    def final_body(*refs):
        final_kernel(n_grp, *refs)

    return call(
        final_body,
        shape((QUANT, MODES, LANES), f32),
        [
            pltpu.VMEM((3 * MODES, QUANT * LANES), bf16),
            pltpu.VMEM((4 * MODES, QUANT * LANES), f32),
            pltpu.VMEM((4, QUANT, MODES, LANES), f32),
        ],
        *gots, partial, near, across, riem, cluster, face_partner, partner_face,
        cohesion.reshape(1, owned), relax_time.reshape(1, owned), yield_flag.reshape(1, owned),
        name="final",
    )


def solution(mesh):
    n_dom, n_grp = mesh.shape["dom"], mesh.shape["grp"]
    both = ("dom", "grp")
    in_specs = (
        P(None, None, both), P(), P(None, None, None, both), P(), P(),
        P(None, None, None, None, both), P(both), P(both), P(None, both), P(None, both),
        P(both), P(both), P(both),
    )

    def body(*args):
        return on_device(n_dom, n_grp, *args)

    return jax.shard_map(
        body, mesh=mesh, in_specs=in_specs, out_specs=P(None, None, both), check_vma=False
    )
```

time: 74.4 us -> 32.6 us (0.44)
  other arithmetic: 22 us -> 0 us
  local copies, waits for them, and re-layouts: 24 us -> 5.1 us
  matrix products: 17 us -> 0 us
  Pallas kernels: 0 us -> 13.5 us
  waiting for transfers between devices: 0.01 us -> 3.26 us
    dot_general x26 -> x0, matrix products: 17 us -> none  [the longest x22 13.2 us: on_modes(): return jnp.einsum('mn,qne->qme', matrix, operand, precision=highest)]
    pallas_call x0 -> x5, Pallas kernels: none -> 13.5 us  [call(): pl.pallas_call(kernel, out_shape=out_shape, in_specs=[vmem] * len(args),...]
    reduce_sum x27 -> x0, other arithmetic: 10.3 us -> none  [the longest x24 7.92 us: on_quantities(): return jnp.sum(operand[:, None, :, :] * blocks[:, :, None, :], axis=0)]
    gather x5 -> x0, local copies, waits for them, and re-layouts: 9.5 us -> none  [the longest x4 7.46 us: on_device(): picked = jnp.take(listing, face_partner[face_index], axis=1)]
    select_n x6 -> x0, other arithmetic: 5.36 us -> none  [the longest x4 5.15 us: on_device(): picked = jnp.take(listing, face_partner[face_index], axis=1)]
    ppermute x2 -> x9, starting transfers between devices: 5.69 us -> 10.4 us  [the longest x5 5.47 us: on_device(): gots[k] = lax.ppermute(outgoing[k], *routes[k])]
    select_n x4 -> x0, local copies, waits for them, and re-layouts: 4.6 us -> none  [on_device(): picked = jnp.take(listing, face_partner[face_index], axis=1)]
    all_to_all x1 -> x0, starting transfers between devices: 4.37 us -> none  [on_device(): lax.all_to_all(outgoing[:, :GRP_SLOTS], 'grp', split_axis=1, concat_axis=...]
  transfers between devices with their start and end apart: 3 -> 9, of which waited for: 0 -> 2; matrix products, arithmetic and copies ran while one was open for 21% -> 0% of each run, Pallas kernels for 0% -> 22%
where the time goes in v1:
time: 32.6 us; the launch traced here: 32.3 us
  Pallas kernels  13.5 us (41%)
  starting transfers between devices  10.4 us (32%)
  local copies, waits for them, and re-layouts  5.1 us (16%)
  waiting for transfers between devices  3.26 us (10%)
    pallas_call x5, Pallas kernels, call(): pl.pallas_call(kernel, out_shape=out_shape, in_specs=[vmem] * len(args),...  13.5 us
    ppermute x5, starting transfers between devices, on_device(): gots[k] = lax.ppermute(outgoing[k], *routes[k])  5.47 us
    unnamed x28, local copies, waits for them, and re-layouts  5.09 us
    ppermute x4, starting transfers between devices, on_device(): wanted[k] = lax.ppermute(requests[k], *routes[k])  4.9 us
    ppermute x5, waiting for transfers between devices, on_device(): gots[k] = lax.ppermute(outgoing[k], *routes[k])  3.25 us
  transfers between devices with their start and end apart: 9, of which 2 were waited for; matrix products, arithmetic and copies ran while one was open for 0% of the time, Pallas kernels for 22%

profile of v1, /device:TPU:0, one launch (start us, length us, event | category | flops | bytes accessed | tf_op | source)
XLA Modules:
  0.0 32.3 jit_solution(7992261837313414203)
XLA Ops:
  0.0 0.0 copy-start.8
  0.0 0.7 %copy-done.8 = s32[128]{0:T(128)S(1)} copy-done((s32[128]{0:T(128)S(1)}, s32[128]{0:T(128)}, u32[]{:S(2)}) %copy-start.8) | copy-done | bytes 536
  0.7 0.0 copy-start.6
  0.7 0.7 %copy-done.6 = s32[4,128]{1,0:T(4,128)S(1)} copy-done((s32[4,128]{1,0:T(4,128)S(1)}, s32[4,128]{1,0:T(4,128)}, u32[]{:S(2)}) %copy-start.6) | copy-done | bytes 2072
  1.3 0.2 requests.1
  1.6 0.5 %collective-permute-start = (s32[8,128]{1,0:T(8,128)S(1)}, s32[8,128]{1,0:T(8,128)S(1)}, u32[]{:S(2)}, u32[]{:S(2)}) collective-permute-start(s32[8,128]{1,0:T(8,128)S(1)} %get-tuple-element.17), channel_id=1, source_target_pairs={{0,1},{1,0},{2,3},{3,2},{4,5},{5,4},{6,7},{7,6},{8,9},{9,8},{10,11... | collective-permute-start | bytes 12296 | tf_op jit(solution)/shard_map/ppermute | solution.py:356
  2.1 0.0 copy-start.13
  2.1 2.6 %collective-permute-start.1 = (s32[8,128]{1,0:T(8,128)S(1)}, s32[8,128]{1,0:T(8,128)S(1)}, u32[]{:S(2)}, u32[]{:S(2)}) collective-permute-start(s32[8,128]{1,0:T(8,128)S(1)} %get-tuple-element.18), channel_id=1, source_target_pairs={{0,2},{1,3},{2,0},{3,1},{4,6},{5,7},{6,4},{7,5},{8,10},{9,11},{10,... | collective-permute-start | bytes 12296 | tf_op jit(solution)/shard_map/ppermute | solution.py:356
  4.7 0.0 collective-permute-start.2
  4.7 1.8 %collective-permute-start.3 = (s32[8,128]{1,0:T(8,128)S(1)}, s32[8,128]{1,0:T(8,128)S(1)}, u32[]{:S(2)}, u32[]{:S(2)}) collective-permute-start(s32[8,128]{1,0:T(8,128)S(1)} %get-tuple-element.20), channel_id=1, source_target_pairs={{0,4},{4,0},{8,12},{12,8},{16,20},{20,16},{24,28},{28,24},{1,5},{5... | collective-permute-start | bytes 12296 | tf_op jit(solution)/shard_map/ppermute | solution.py:356
  6.5 0.0 copy-done.13
  6.5 0.0 copy-start.1
  6.5 0.9 %copy-done.1 = f32[9,56,128]{2,1,0:T(8,128)S(1)} copy-done((f32[9,56,128]{2,1,0:T(8,128)S(1)}, f32[9,56,128]{2,1,0:T(8,128)}, u32[]{:S(2)}) %copy-start.1) | copy-done | bytes 258072
  7.4 0.0 copy-start.2
  7.4 0.9 %copy-done.2 = f32[3,9,9,128]{3,0,2,1:T(4,128)S(1)} copy-done((f32[3,9,9,128]{3,0,2,1:T(4,128)S(1)}, f32[3,9,9,128]{3,0,2,1:T(4,128)}, u32[]{:S(2)}) %copy-start.2) | copy-done | bytes 124440
  8.3 0.0 copy-start.4
  8.3 0.9 %copy-done.4 = f32[3,56,56]{2,1,0:T(8,128)S(1)} copy-done((f32[3,56,56]{2,1,0:T(8,128)S(1)}, f32[3,56,56]{2,1,0:T(8,128)}, u32[]{:S(2)}) %copy-start.4) | copy-done | bytes 37656
  9.2 0.0 copy-start.5
  9.2 4.3 %predictor.1.refs_0_ = f32[1536,128]{1,0:T(8,128)S(1)} custom-call(f32[9,56,128]{2,1,0:T(8,128)S(1)} %copy-done.1, f32[3,56,56]{2,1,0:T(8,128)S(1)} %copy-done.4, f32[9,9,3,128]{3,2,1,0:T(4,128)S(1)} %bitcast.8), custom_call_target="tpu_custom_call" | custom-call | tf_op jit(solution)/shard_map/predictor/pallas_call | solution.py:313
  13.6 0.0 copy-start
  13.6 0.0 copy-start.3
  13.6 0.0 collective-permute-done.refs_2_
  13.6 0.0 collective-permute-done.1.refs_3_
  13.6 0.0 collective-permute-done.2.refs_4_
  13.6 0.0 collective-permute-done.3.refs_5_
  13.6 1.5 %sends.1 = (f32[256,128]{1,0:T(8,128)S(1)}, f32[256,128]{1,0:T(8,128)S(1)}, f32[256,128]{1,0:T(8,128)S(1)}, f32[128,128]{1,0:T(8,128)S(1)}, f32[384,128]{1,0:T(8,128)S(1)}) custom-call(f32[1536,128]{1,0:T(8,128)S(1)} %predictor.1.refs_0_, s32[1,320]{1,0:T(1,128)S(1)} %reshape.15.refs_1_.refs_8_, s32[8,128]{1,0:T(8,128)S(1)} %collective-permute-done.refs_2_, ...), custom_call_target="tpu_custom_call" | custom-call | tf_op jit(solution)/shard_map/sends/pallas_call | solution.py:313
  15.1 3.6 %collective-permute-start.8 = (f32[384,128]{1,0:T(8,128)S(1)}, f32[384,128]{1,0:T(8,128)S(1)}, u32[]{:S(2)}, u32[]{:S(2)}) collective-permute-start(f32[384,128]{1,0:T(8,128)S(1)} %get-tuple-element.25), channel_id=1, source_target_pairs={{0,28},{4,8},{8,4},{12,16},{16,12},{20,24},{24,20},{28,0},{1,29},{... | collective-permute-start | bytes 589832 | tf_op jit(solution)/shard_map/ppermute | solution.py:384
  18.7 0.0 collective-permute-start.4
  18.7 1.5 %collective-permute-start.5 = (f32[256,128]{1,0:T(8,128)S(1)}, f32[256,128]{1,0:T(8,128)S(1)}, u32[]{:S(2)}, u32[]{:S(2)}) collective-permute-start(f32[256,128]{1,0:T(8,128)S(1)} %get-tuple-element.22), channel_id=1, source_target_pairs={{0,2},{1,3},{2,0},{3,1},{4,6},{5,7},{6,4},{7,5},{8,10},{9,11},{10,... | collective-permute-start | bytes 393224 | tf_op jit(solution)/shard_map/ppermute | solution.py:384
  20.2 0.0 copy-start.7
  20.2 0.4 %collective-permute-start.6 = (f32[256,128]{1,0:T(8,128)S(1)}, f32[256,128]{1,0:T(8,128)S(1)}, u32[]{:S(2)}, u32[]{:S(2)}) collective-permute-start(f32[256,128]{1,0:T(8,128)S(1)} %get-tuple-element.23), channel_id=1, source_target_pairs={{0,3},{1,2},{2,1},{3,0},{4,7},{5,6},{6,5},{7,4},{8,11},{9,10},{10,... | collective-permute-start | bytes 393224 | tf_op jit(solution)/shard_map/ppermute | solution.py:384
  20.6 0.0 collective-permute-start.7
  20.6 0.0 copy-done.5
  20.6 0.0 copy-done
  20.6 0.0 copy-done.3
  20.6 0.3 copy-done.7
  20.9 2.8 %own.1 = (f32[9,56,128]{2,1,0:T(8,128)S(1)}, f32[4,504,128]{2,1,0:T(8,128)S(1)}, bf16[4,224,168]{2,1,0:T(8,128)(2,1)S(1)}) custom-call(f32[1536,128]{1,0:T(8,128)S(1)} %predictor.1.refs_0_, f32[9,56,128]{2,1,0:T(8,128)S(1)} %copy-done.1, f32[3,56,56]{2,1,0:T(8,128)S(1)} %copy-done.4, f32[9,9,3,128]{3,2,1,0:T(4,128)S(1)} %bitcast.9, ...), custom_call_target="tpu_custom_call" | custom-call | flops 100000000 | bytes 4000000 | tf_op jit(solution)/shard_map/own/pallas_call | solution.py:313
  23.7 2.4 %collective-permute-done.7.refs_3_ = f32[128,128]{1,0:T(8,128)S(1)} collective-permute-done((f32[128,128]{1,0:T(8,128)S(1)}, f32[128,128]{1,0:T(8,128)S(1)}, u32[]{:S(2)}, u32[]{:S(2)}) %collective-permute-start.7) | collective-permute-done | bytes 65568 | tf_op jit(solution)/shard_map/ppermute | solution.py:384
  26.2 0.0 collective-permute-done.4.refs_0_
  26.2 0.0 collective-permute-done.5.refs_1_
  26.2 0.8 %collective-permute-done.6.refs_2_ = f32[256,128]{1,0:T(8,128)S(1)} collective-permute-done((f32[256,128]{1,0:T(8,128)S(1)}, f32[256,128]{1,0:T(8,128)S(1)}, u32[]{:S(2)}, u32[]{:S(2)}) %collective-permute-start.6) | collective-permute-done | bytes 131104 | tf_op jit(solution)/shard_map/ppermute | solution.py:384
  27.0 0.0 collective-permute-done.8.refs_4_
  27.0 0.0 copy-start.9
  27.0 0.0 copy-start.10
  27.0 0.0 copy-start.11
  27.0 0.0 copy-start.12
  27.0 0.7 %copy-done.9 = s32[4,128]{1,0:T(4,128)S(1)} copy-done((s32[4,128]{1,0:T(4,128)S(1)}, s32[4,128]{1,0:T(4,128)}, u32[]{:S(2)}) %copy-start.9) | copy-done | bytes 2072
  27.7 0.0 copy-done.10
  27.7 0.0 copy-done.11
  27.7 0.0 copy-done.12
  27.7 4.7 %final.1 = f32[9,56,128]{2,1,0:T(8,128)} custom-call(f32[256,128]{1,0:T(8,128)S(1)} %collective-permute-done.4.refs_0_, f32[256,128]{1,0:T(8,128)S(1)} %collective-permute-done.5.refs_1_, f32[256,128]{1,0:T(8,128)S(1)} %collective-permute-done.6.refs_2_, f32[128,128]{1,0:T(8,128)S(1)} %collective-permute-done.7.refs_3_, ...), custom_call_target="tpu_custom_call" | custom-call | tf_op jit(solution)/shard_map/final/pallas_call | solution.py:313
  (1 shorter events, 0.0 us)
Async XLA Ops:
  0.0 0.7 %copy-start.8 = (s32[128]{0:T(128)S(1)}, s32[128]{0:T(128)}, u32[]{:S(2)}) copy-start(s32[128]{0:T(128)} %param.19) | copy-start | bytes 1540
  0.7 0.7 %copy-start.6 = (s32[4,128]{1,0:T(4,128)S(1)}, s32[4,128]{1,0:T(4,128)}, u32[]{:S(2)}) copy-start(s32[4,128]{1,0:T(4,128)} %refs_10_.1) | copy-start | bytes 6148
  1.6 12.0 %collective-permute-start = (s32[8,128]{1,0:T(8,128)S(1)}, s32[8,128]{1,0:T(8,128)S(1)}, u32[]{:S(2)}, u32[]{:S(2)}) collective-permute-start(s32[8,128]{1,0:T(8,128)S(1)} %get-tuple-element.17), channel_id=1, source_target_pairs={{0,1},{1,0},{2,3},{3,2},{4,5},{5,4},{6,7},{7,6},{8,9},{9,8},{10,11... | collective-permute-start | bytes 12296 | tf_op jit(solution)/shard_map/ppermute | solution.py:356
  2.1 4.4 %copy-start.13 = (s32[320]{0:T(512)S(1)}, s32[320]{0:T(512)}, u32[]{:S(2)}) copy-start(s32[320]{0:T(512)} %param.20) | copy-start | bytes 3844
  2.1 11.5 %collective-permute-start.1 = (s32[8,128]{1,0:T(8,128)S(1)}, s32[8,128]{1,0:T(8,128)S(1)}, u32[]{:S(2)}, u32[]{:S(2)}) collective-permute-start(s32[8,128]{1,0:T(8,128)S(1)} %get-tuple-element.18), channel_id=1, source_target_pairs={{0,2},{1,3},{2,0},{3,1},{4,6},{5,7},{6,4},{7,5},{8,10},{9,11},{10,... | collective-permute-start | bytes 12296 | tf_op jit(solution)/shard_map/ppermute | solution.py:356
  4.7 9.0 %collective-permute-start.2 = (s32[8,128]{1,0:T(8,128)S(1)}, s32[8,128]{1,0:T(8,128)S(1)}, u32[]{:S(2)}, u32[]{:S(2)}) collective-permute-start(s32[8,128]{1,0:T(8,128)S(1)} %get-tuple-element.19), channel_id=1, source_target_pairs={{0,3},{1,2},{2,1},{3,0},{4,7},{5,6},{6,5},{7,4},{8,11},{9,10},{10,... | collective-permute-start | bytes 12296 | tf_op jit(solution)/shard_map/ppermute | solution.py:356
  4.7 8.9 %collective-permute-start.3 = (s32[8,128]{1,0:T(8,128)S(1)}, s32[8,128]{1,0:T(8,128)S(1)}, u32[]{:S(2)}, u32[]{:S(2)}) collective-permute-start(s32[8,128]{1,0:T(8,128)S(1)} %get-tuple-element.20), channel_id=1, source_target_pairs={{0,4},{4,0},{8,12},{12,8},{16,20},{20,16},{24,28},{28,24},{1,5},{5... | collective-permute-start | bytes 12296 | tf_op jit(solution)/shard_map/ppermute | solution.py:356
  6.5 0.9 %copy-start.1 = (f32[9,56,128]{2,1,0:T(8,128)S(1)}, f32[9,56,128]{2,1,0:T(8,128)}, u32[]{:S(2)}) copy-start(f32[9,56,128]{2,1,0:T(8,128)} %refs_1_.1) | copy-start | bytes 774148
  7.4 0.9 %copy-start.2 = (f32[3,9,9,128]{3,0,2,1:T(4,128)S(1)}, f32[3,9,9,128]{3,0,2,1:T(4,128)}, u32[]{:S(2)}) copy-start(f32[3,9,9,128]{3,0,2,1:T(4,128)} %param.15) | copy-start | bytes 373252
  8.3 0.9 %copy-start.4 = (f32[3,56,56]{2,1,0:T(8,128)S(1)}, f32[3,56,56]{2,1,0:T(8,128)}, u32[]{:S(2)}) copy-start(f32[3,56,56]{2,1,0:T(8,128)} %refs_2_.1) | copy-start | bytes 112900
  9.2 11.4 %copy-start.5 = (f32[4,56,56]{2,1,0:T(8,128)S(1)}, f32[4,56,56]{2,1,0:T(8,128)}, u32[]{:S(2)}) copy-start(f32[4,56,56]{2,1,0:T(8,128)} %refs_4_.1) | copy-start | bytes 150532
  13.6 7.0 %copy-start = (f32[2,4,9,9,128]{4,1,3,2,0:T(4,128)S(1)}, f32[2,4,9,9,128]{4,1,3,2,0:T(4,128)}, u32[]{:S(2)}) copy-start(f32[2,4,9,9,128]{4,1,3,2,0:T(4,128)} %param.18) | copy-start | bytes 995332
  13.6 7.0 %copy-start.3 = (f32[4,4,56,56]{3,2,1,0:T(8,128)S(1)}, f32[4,4,56,56]{3,2,1,0:T(8,128)}, u32[]{:S(2)}) copy-start(f32[4,4,56,56]{3,2,1,0:T(8,128)} %refs_5_.1) | copy-start | bytes 602116
  15.1 11.9 %collective-permute-start.8 = (f32[384,128]{1,0:T(8,128)S(1)}, f32[384,128]{1,0:T(8,128)S(1)}, u32[]{:S(2)}, u32[]{:S(2)}) collective-permute-start(f32[384,128]{1,0:T(8,128)S(1)} %get-tuple-element.25), channel_id=1, source_target_pairs={{0,28},{4,8},{8,4},{12,16},{16,12},{20,24},{24,20},{28,0},{1,29},{... | collective-permute-start | bytes 589832 | tf_op jit(solution)/shard_map/ppermute | solution.py:384
  18.7 7.5 %collective-permute-start.4 = (f32[256,128]{1,0:T(8,128)S(1)}, f32[256,128]{1,0:T(8,128)S(1)}, u32[]{:S(2)}, u32[]{:S(2)}) collective-permute-start(f32[256,128]{1,0:T(8,128)S(1)} %get-tuple-element.21), channel_id=1, source_target_pairs={{0,1},{1,0},{2,3},{3,2},{4,5},{5,4},{6,7},{7,6},{8,9},{9,8},{10,11... | collective-permute-start | bytes 393224 | tf_op jit(solution)/shard_map/ppermute | solution.py:384
  18.7 7.5 %collective-permute-start.5 = (f32[256,128]{1,0:T(8,128)S(1)}, f32[256,128]{1,0:T(8,128)S(1)}, u32[]{:S(2)}, u32[]{:S(2)}) collective-permute-start(f32[256,128]{1,0:T(8,128)S(1)} %get-tuple-element.22), channel_id=1, source_target_pairs={{0,2},{1,3},{2,0},{3,1},{4,6},{5,7},{6,4},{7,5},{8,10},{9,11},{10,... | collective-permute-start | bytes 393224 | tf_op jit(solution)/shard_map/ppermute | solution.py:384
  20.2 0.7 %copy-start.7 = (s32[4,128]{1,0:T(4,128)S(1)}, s32[4,128]{1,0:T(4,128)}, u32[]{:S(2)}) copy-start(s32[4,128]{1,0:T(4,128)} %refs_10_.1) | copy-start | bytes 6148
  20.2 6.8 %collective-permute-start.6 = (f32[256,128]{1,0:T(8,128)S(1)}, f32[256,128]{1,0:T(8,128)S(1)}, u32[]{:S(2)}, u32[]{:S(2)}) collective-permute-start(f32[256,128]{1,0:T(8,128)S(1)} %get-tuple-element.23), channel_id=1, source_target_pairs={{0,3},{1,2},{2,1},{3,0},{4,7},{5,6},{6,5},{7,4},{8,11},{9,10},{10,... | collective-permute-start | bytes 393224 | tf_op jit(solution)/shard_map/ppermute | solution.py:384
  20.6 5.6 %collective-permute-start.7 = (f32[128,128]{1,0:T(8,128)S(1)}, f32[128,128]{1,0:T(8,128)S(1)}, u32[]{:S(2)}, u32[]{:S(2)}) collective-permute-start(f32[128,128]{1,0:T(8,128)S(1)} %get-tuple-element.24), channel_id=1, source_target_pairs={{0,4},{4,0},{8,12},{12,8},{16,20},{20,16},{24,28},{28,24},{1,5},{5... | collective-permute-start | bytes 196616 | tf_op jit(solution)/shard_map/ppermute | solution.py:384
  27.0 0.7 %copy-start.9 = (s32[4,128]{1,0:T(4,128)S(1)}, s32[4,128]{1,0:T(4,128)}, u32[]{:S(2)}) copy-start(s32[4,128]{1,0:T(4,128)} %refs_11_.1) | copy-start | bytes 6148
  27.0 0.7 %copy-start.10 = (f32[128]{0:T(128)S(1)}, f32[128]{0:T(128)}, u32[]{:S(2)}) copy-start(f32[128]{0:T(128)} %param.23) | copy-start | bytes 1540
  27.0 0.7 %copy-start.11 = (f32[128]{0:T(128)S(1)}, f32[128]{0:T(128)}, u32[]{:S(2)}) copy-start(f32[128]{0:T(128)} %param.24) | copy-start | bytes 1540
  27.0 0.7 %copy-start.12 = (s32[128]{0:T(128)S(1)}, s32[128]{0:T(128)}, u32[]{:S(2)}) copy-start(s32[128]{0:T(128)} %param.25) | copy-start | bytes 1540

commit v2 on v1

v2 whole, which is shorter than its diff:
```python
import jax
import jax.numpy as jnp
from jax import lax
from jax.experimental import pallas as pl
from jax.experimental.pallas import tpu as pltpu
from jax.sharding import PartitionSpec as P

QUANT = 9
MODES = 56
ORDER = 6
GRP_SLOTS = 256
HALO = 32
LEVELS = 3
LANES = 128
SUB = 8
MT = MODES // SUB
VT = QUANT * MT
VP = 64
GROUP = 3

base_step = 0.2
f32 = jnp.float32
bf16 = jnp.bfloat16
i32 = jnp.int32
VMEM_LIMIT = 24 << 20


def round_up(value, unit):
    return -(-value // unit) * unit


class Plan:
    def __init__(self, n_dom, n_grp):
        share = GRP_SLOTS // n_grp
        self.n_grp = n_grp
        self.width = [HALO, HALO] + [share] * (n_grp - 1)
        pairs = [(i, i ^ 1) for i in range(n_dom)]
        others = [(i, ((i + 1) if i % 2 else (i - 1)) % n_dom) for i in range(n_dom)]
        self.route = [("dom", pairs), ("dom", others)]
        self.route += [("grp", [(i, i ^ k) for i in range(n_grp)]) for k in range(1, n_grp)]
        self.reg, self.start = [], []
        at = 0
        for w in self.width:
            at = round_up(at, w)
            self.reg.append(at // LANES)
            self.start.append(at % LANES)
            at += w
        self.n_reg = -(-at // LANES)
        self.count = len(self.width)
        self.full = [k == 1 for k in range(self.count)]
        narrow = min(self.width)
        self.shift = narrow.bit_length() - 1
        self.masks = LANES // narrow
        self.order = [k for k in range(3, self.count)] + [0, 2]

    def chunk(self, k):
        return VP * self.width[k] // LANES

    def height(self, k):
        return self.chunk(k) * (LEVELS if self.full[k] else 1)

    def mask_id(self, v):
        return v * self.masks // VP

    def members(self, reg):
        return [k for k in range(self.count) if self.reg[k] == reg]

    def bases(self):
        grp = lax.axis_index("grp")
        odd = jnp.bitwise_and(lax.axis_index("dom"), 1)
        found = [GRP_SLOTS + HALO * (1 - odd), GRP_SLOTS + HALO * odd]
        for k in range(1, self.n_grp):
            found.append(jnp.bitwise_xor(grp, k) * self.width[k + 1])
        return found


def take(x, idx):
    flat = x.reshape(-1, LANES)
    wide = jnp.broadcast_to(idx[None], (flat.shape[0] // SUB, SUB, LANES)).reshape(flat.shape)
    out = jnp.take_along_axis(flat, wide, axis=1, mode="promise_in_bounds")
    return out.reshape(x.shape)


def pick(ref, position):
    lane = jnp.bitwise_and(position, LANES - 1)
    tile = jnp.right_shift(position, 7)
    out = take(ref[:, 0:LANES], lane)
    for v in range(1, ref.shape[1] // LANES):
        out = jnp.where(tile == v, take(ref[:, v * LANES : (v + 1) * LANES], lane), out)
    return out


def lane_ids():
    return lax.broadcasted_iota(i32, (SUB, LANES), 1)


def spread(row):
    return jnp.broadcast_to(row, (SUB, row.shape[-1]))


def split(x):
    high = x.astype(bf16).astype(f32)
    return high, x - high


def stationary(x):
    high, low = split(x.reshape(MODES, x.shape[-1]))
    return jnp.concatenate([high, low, high], axis=0).astype(bf16)


def streamed(w):
    high, low = split(w)
    return jnp.concatenate([high, high, low], axis=1).astype(bf16)


def matmul(w, x):
    return jnp.dot(w, x, preferred_element_type=f32)


def row8(ref, index, sub):
    return spread(ref[(*index, pl.ds(sub, 1), slice(None))])


def quantity(q):
    return pl.ds(q * MT, MT)


def request_kernel(plan, *refs):
    n_load = 3
    partner_hbm, cluster_hbm = refs[0:2]
    bulk_hbm = refs[2 : 2 + n_load]
    rest = refs[2 + n_load :]
    outs, rest = rest[: plan.count], rest[plan.count :]
    bulk_out, rest = rest[:n_load], rest[n_load:]
    partner_ref, cluster_ref, row_ref, sems = rest
    copies = [
        pltpu.make_async_copy(partner_hbm, partner_ref, sems.at[0]),
        pltpu.make_async_copy(cluster_hbm, cluster_ref, sems.at[1]),
    ]
    copies += [
        pltpu.make_async_copy(a, b, sems.at[2 + i]) for i, (a, b) in enumerate(zip(bulk_hbm, bulk_out))
    ]
    for copy in copies:
        copy.start()
    for copy in copies[:2]:
        copy.wait()
    received = GRP_SLOTS + 2 * HALO
    owned = cluster_ref.shape[1]
    place = lax.broadcasted_iota(i32, (received, LANES), 0) + owned
    cluster = cluster_ref[...].astype(f32)
    marks = jnp.zeros((received, LANES), f32)
    for f in range(4):
        marks = jnp.where(partner_ref[f : f + 1, :] == place, cluster, marks)
    rows = lax.dot_general(
        jnp.ones((SUB, LANES), bf16),
        marks.astype(bf16),
        (((1,), (1,)), ((), ())),
        preferred_element_type=f32,
    )
    row_ref[...] = jnp.zeros(row_ref.shape, i32)
    row_ref[:, :received] = rows.astype(i32)
    lane = lane_ids()
    for out, base, width in zip(outs, plan.bases(), plan.width):
        out[...] = pick(row_ref, base + jnp.bitwise_and(lane, width - 1))
    for copy in copies[2:]:
        copy.wait()


def predictor_kernel(state_ref, stiff_ref, jac_ref, level_ref, w_ref, rhs_ref, y0_ref, y1_ref):
    w_ref[...] = streamed(stiff_ref[...].reshape(3 * MODES, MODES))
    level_ref[:, pl.ds(VT, VP - VT)] = jnp.zeros((LEVELS, VP - VT, SUB, LANES), f32)
    steps = QUANT // GROUP

    def project(y_ref, g):
        y = matmul(w_ref[...], rhs_ref[g])
        for i in range(GROUP):
            y_ref[g, i] = y[:, i * LANES : (i + 1) * LANES].reshape(3 * MT, SUB, LANES)

    for q in range(QUANT):
        v = state_ref[q].reshape(MT, SUB, LANES) * base_step
        rhs_ref[1 + q // GROUP, :, pl.ds(q % GROUP * LANES, LANES)] = stationary(v)
        for c in range(LEVELS):
            level_ref[c, quantity(q)] = v * 2.0**c
    for g in range(steps):
        project(y0_ref, g + 1)
    for degree in range(1, ORDER):
        y_ref, next_ref = (y0_ref, y1_ref) if degree % 2 == 1 else (y1_ref, y0_ref)
        factor = -base_step / (degree + 1)
        last = degree == ORDER - 1

        def body(g, carry, y_ref=y_ref, next_ref=next_ref, factor=factor, last=last, degree=degree):
            if not last:
                project(next_ref, g)
            acc = [None] * GROUP
            for p in range(QUANT):
                for d in range(3):
                    y = y_ref[1 + p // GROUP, p % GROUP, pl.ds(d * MT, MT)]
                    for i in range(GROUP):
                        term = y * row8(jac_ref, (p, g * GROUP + i), d)
                        acc[i] = term if acc[i] is None else acc[i] + term
            for i in range(GROUP):
                v = acc[i] * factor
                at = pl.ds((g * GROUP + i) * MT, MT)
                for c in range(LEVELS):
                    level_ref[c, at] = level_ref[c, at] + v * 2.0 ** (c * (degree + 1))
                if not last:
                    rhs_ref[g + 1, :, pl.ds(i * LANES, LANES)] = stationary(v)
            return carry

        lax.fori_loop(0, steps, body, 0)
        if not last:
            project(next_ref, steps)


def send_kernel(plan, reg, level_ref, slot_ref, *rest):
    mine = plan.members(reg)
    asked = [k for k in mine if not plan.full[k]]
    reqs = dict(zip(asked, rest[: len(asked)]))
    outs = dict(zip(mine, rest[len(asked) : -1]))
    row_ref = rest[-1]
    row_ref[...] = jnp.zeros(row_ref.shape, i32)
    row_ref[:, : slot_ref.shape[1]] = spread(slot_ref[...])
    lane = lane_ids()
    bases = plan.bases()
    index = jnp.zeros((SUB, LANES), i32)
    want = jnp.zeros((SUB, LANES), i32)
    for k in mine:
        w = plan.width[k]
        inside = jnp.right_shift(lane, w.bit_length() - 1) == plan.start[k] // w
        index = jnp.where(inside, pick(row_ref, bases[k] + jnp.bitwise_and(lane, w - 1)), index)
        if k in reqs:
            want = jnp.where(inside, reqs[k][...], want)
    swap = [jnp.bitwise_xor(lane, m << plan.shift) for m in range(plan.masks)]
    indices = [index] + [take(index, s) for s in swap[1:]]
    wants = [want] + [take(want, s) for s in swap[1:]]
    block = {k: jnp.right_shift(lane, plan.width[k].bit_length() - 1) for k in mine}
    widest = max(plan.chunk(k) for k in mine)
    narrowest = min(plan.chunk(k) for k in mine)
    for u in range(narrowest):
        plain, chosen = {}, {}
        for v in range(u, VP, narrowest):
            m = plan.mask_id(v)
            plain[v] = [take(level_ref[c, v], indices[m]) for c in range(LEVELS)]
            got = plain[v][0]
            for c in range(1, LEVELS):
                got = jnp.where(wants[m] == c, plain[v][c], got)
            chosen[v] = got
        for k in mine:
            chunk = plan.chunk(k)
            n_block = LANES // plan.width[k]
            first = plan.start[k] // plan.width[k]
            for w in range(u, chunk, narrowest):
                for c in range(LEVELS if plan.full[k] else 1):
                    out = None
                    for j in range(n_block):
                        v = (j ^ first) * chunk + w
                        part = plain[v][c] if plan.full[k] else chosen[v]
                        out = part if out is None else jnp.where(block[k] == j, part, out)
                    outs[k][c * chunk + w] = out


def own_kernel(
    plan, level_ref, state_ref, stiff_ref, jac_ref, lift_ref, across_ref, riem_ref,
    cluster_ref, slot_ref, partner_ref, relax_ref, yield_ref,
    part_ref, near_ref, wa_ref, gain_ref,
    row_ref, w_ref, rhs_ref, y_ref,
):
    cluster = spread(cluster_ref[...])
    for q in range(QUANT):
        own = level_ref[0, quantity(q)]
        for c in range(1, LEVELS):
            own = jnp.where((cluster == c)[None], level_ref[c, quantity(q)], own)
        rhs_ref[:, pl.ds(q * LANES, LANES)] = stationary(own)
    for d in range(3):
        w_ref[pl.ds(d * MODES, MODES), :] = streamed(stiff_ref[d].T)
    w_ref[pl.ds(3 * MODES, 4 * MODES), :] = streamed(lift_ref[...].reshape(4 * MODES, MODES))
    y = matmul(w_ref[...], rhs_ref[...])
    for q in range(QUANT):
        y_ref[q] = y[:, q * LANES : (q + 1) * LANES].reshape(7 * MT, SUB, LANES)

    def gather(q, carry):
        acc = state_ref[q].reshape(MT, SUB, LANES)
        for p in range(QUANT):
            for d in range(3):
                acc = acc + y_ref[p, pl.ds(d * MT, MT)] * row8(jac_ref, (p, q), d)
            for f in range(4):
                acc = acc - y_ref[p, pl.ds((3 + f) * MT, MT)] * row8(riem_ref, (0, p, q), f)
        part_ref[pl.ds(q * MT, MT)] = acc
        return carry

    lax.fori_loop(0, QUANT, gather, 0)
    row_ref[...] = jnp.zeros(row_ref.shape, i32)
    row_ref[:, : slot_ref.shape[1]] = spread(slot_ref[...])
    owned = cluster_ref.shape[1]
    for f in range(4):
        place = spread(partner_ref[f : f + 1, :])
        slot = jnp.maximum(place - owned, 0)
        idx = jnp.where(place < owned, place, pick(row_ref, slot))

        def local(q, carry, idx=idx, f=f):
            at = pl.ds(q * MT, MT)
            near = take(level_ref[0, at], idx)
            for c in range(1, LEVELS):
                near = jnp.where((cluster == c)[None], take(level_ref[c, at], idx), near)
            near_ref[f, at] = near
            return carry

        lax.fori_loop(0, QUANT, local, 0)
        wa_ref[f] = streamed(across_ref[f].reshape(4 * MODES, MODES))
    step = jnp.where(cluster == 0, base_step, jnp.where(cluster == 1, 2.0 * base_step, 4.0 * base_step))
    gain_ref[...] = spread(yield_ref[...].astype(f32)) * (1.0 - jnp.exp(-step / spread(relax_ref[...])))


def final_kernel(plan, *refs):
    gots = refs[: plan.count]
    (wish_ref, part_ref, near_ref, wa_ref, riem_ref, partner_ref, side_ref,
     cohesion_ref, gain_ref, out_ref, mixed_ref, rhs_ref, z_ref, chosen_ref) = refs[plan.count :]
    owned = partner_ref.shape[1]
    lane = lane_ids()
    bases = plan.bases()
    wishes = [
        wish_ref[...] if m == 0 else take(wish_ref[...], jnp.bitwise_xor(lane, m << plan.shift))
        for m in range(plan.masks)
    ]
    for r in range(plan.n_reg):
        mine = plan.members(r)
        block = {k: jnp.right_shift(lane, plan.width[k].bit_length() - 1) for k in mine}
        for v in range(VT):
            mixed = None
            for k in mine:
                chunk = plan.chunk(k)
                got = gots[k][v % chunk]
                if plan.full[k]:
                    for c in range(1, LEVELS):
                        got = jnp.where(wishes[plan.mask_id(v)] == c, gots[k][c * chunk + v % chunk], got)
                at = (plan.start[k] // plan.width[k]) ^ (v // chunk)
                mixed = got if mixed is None else jnp.where(block[k] == at, got, mixed)
            mixed_ref[r, v] = mixed
    for f in range(4):
        slot = spread(partner_ref[f : f + 1, :]) - owned
        spot = jnp.zeros((SUB, LANES), i32)
        where = jnp.zeros((SUB, LANES), i32) - 1
        for k in range(plan.count):
            rel = slot - bases[k]
            hit = jnp.logical_and(rel >= 0, rel < plan.width[k])
            spot = jnp.where(hit, rel + plan.start[k], spot)
            where = jnp.where(hit, plan.reg[k], where)
        spots = [jnp.bitwise_xor(spot, m << plan.shift) for m in range(plan.masks)]
        side = spread(side_ref[f : f + 1, :])
        for q in range(QUANT):
            parts = []
            for v in range(q * MT, (q + 1) * MT):
                near = near_ref[f, v]
                for r in range(plan.n_reg):
                    near = jnp.where(where == r, take(mixed_ref[r, v], spots[plan.mask_id(v)]), near)
                parts.append(near)
            rhs_ref[f, :, pl.ds(q * LANES, LANES)] = stationary(jnp.stack(parts))
        z = matmul(wa_ref[f], rhs_ref[f])
        for q in range(QUANT):
            column = z[:, q * LANES : (q + 1) * LANES].reshape(4, MT, SUB, LANES)
            chosen = column[0]
            for j in range(1, 4):
                chosen = jnp.where((side == j)[None], column[j], chosen)
            chosen_ref[f, q] = chosen

    def gather(q, carry):
        acc = part_ref[pl.ds(q * MT, MT)]
        for f in range(4):
            for p in range(QUANT):
                acc = acc - chosen_ref[f, p] * row8(riem_ref, (1, p, q), f)
        out_ref[q] = acc.reshape(MODES, LANES)
        return carry

    lax.fori_loop(0, QUANT, gather, 0)
    heads = [out_ref[q, 0:1, :] for q in range(6)]
    mean = (heads[0] + heads[1] + heads[2]) / 3.0
    dev = [heads[q] - mean if q < 3 else heads[q] for q in range(6)]
    second = 0.5 * (dev[0] * dev[0] + dev[1] * dev[1] + dev[2] * dev[2])
    second = second + dev[3] * dev[3] + dev[4] * dev[4] + dev[5] * dev[5]
    strength = jnp.sqrt(second)
    cohesion = cohesion_ref[...]
    excess = jnp.maximum(strength - cohesion, 0.0) / jnp.maximum(strength, cohesion)
    factor = spread(gain_ref[0:1, :] * excess)
    now = [out_ref[q].reshape(MT, SUB, LANES) for q in range(6)]
    pressure = (now[0] + now[1] + now[2]) / 3.0
    for q in range(6):
        fresh = now[q] - factor * (now[q] - pressure if q < 3 else now[q])
        out_ref[q] = fresh.reshape(MODES, LANES)


def call(kernel, plan, out_shape, scratch, *args, spaces=None, cost=None, name=None):
    vmem = pl.BlockSpec(memory_space=pltpu.VMEM)
    many = isinstance(out_shape, (list, tuple))

    def body(*refs):
        if plan is None:
            kernel(*refs)
        else:
            kernel(plan, *refs)

    return pl.pallas_call(
        body,
        out_shape=out_shape,
        in_specs=spaces or [vmem] * len(args),
        out_specs=[vmem] * len(out_shape) if many else vmem,
        scratch_shapes=scratch,
        compiler_params=pltpu.CompilerParams(vmem_limit_bytes=VMEM_LIMIT),
        cost_estimate=cost,
        name=name,
    )(*args)


def on_device(
    n_dom, n_grp, old_state, stiffness, jacobians, lift_own, lift_across, riemann,
    cluster_ids, send_slots, face_partner, partner_face, cohesion, relax_time, yield_flag,
):
    plan = Plan(n_dom, n_grp)
    owned = old_state.shape[2]
    slots = send_slots.shape[0]
    wide = round_up(slots, LANES)
    shape = jax.ShapeDtypeStruct
    jac = jnp.transpose(jacobians, (1, 2, 0, 3))
    riem = jnp.transpose(riemann, (0, 2, 3, 1, 4))
    cluster = cluster_ids.reshape(1, owned)
    slot_row = send_slots.reshape(1, slots)
    bulk = (old_state, stiffness, jac)

    early = (face_partner, cluster, *bulk)
    loaded = call(
        request_kernel, plan,
        [shape((SUB, LANES), i32)] * plan.count + [shape(a.shape, a.dtype) for a in bulk],
        [
            pltpu.VMEM(face_partner.shape, i32),
            pltpu.VMEM(cluster.shape, i32),
            pltpu.VMEM((SUB, wide), i32),
            pltpu.SemaphoreType.DMA((len(early),)),
        ],
        *early, spaces=[pl.BlockSpec(memory_space=pl.ANY)] * len(early), name="requests",
    )
    requests, (state_v, stiff_v, jac_v) = loaded[: plan.count], loaded[plan.count :]
    wanted = {}
    for k in plan.order:
        wanted[k] = lax.ppermute(requests[k], *plan.route[k])

    levels = call(
        predictor_kernel, None,
        shape((LEVELS, VP, SUB, LANES), f32),
        [
            pltpu.VMEM((3 * MODES, 3 * MODES), bf16),
            pltpu.VMEM((QUANT // GROUP + 1, 3 * MODES, GROUP * LANES), bf16),
            pltpu.VMEM((QUANT // GROUP + 1, GROUP, 3 * MT, SUB, LANES), f32),
            pltpu.VMEM((QUANT // GROUP + 1, GROUP, 3 * MT, SUB, LANES), f32),
        ],
        state_v, stiff_v, jac_v, name="predictor",
    )

    gots = [None] * plan.count
    for r in reversed(range(plan.n_reg)):
        mine = plan.members(r)
        asked = [wanted[k] for k in mine if not plan.full[k]]
        outgoing = call(
            lambda p, *refs, r=r: send_kernel(p, r, *refs), plan,
            [shape((plan.height(k), SUB, LANES), f32) for k in mine],
            [pltpu.VMEM((SUB, wide), i32)],
            levels, slot_row, *asked, name=f"sends_{r}",
        )
        for k, message in zip(mine, outgoing):
            gots[k] = lax.ppermute(message, *plan.route[k])

    partial, near, across, gain = call(
        own_kernel, plan,
        [
            shape((VT, SUB, LANES), f32),
            shape((4, VT, SUB, LANES), f32),
            shape((4, 4 * MODES, 3 * MODES), bf16),
            shape((SUB, LANES), f32),
        ],
        [
            pltpu.VMEM((SUB, wide), i32),
            pltpu.VMEM((7 * MODES, 3 * MODES), bf16),
            pltpu.VMEM((3 * MODES, QUANT * LANES), bf16),
            pltpu.VMEM((QUANT, 7 * MT, SUB, LANES), f32),
        ],
        levels, state_v, stiff_v, jac_v, lift_own, lift_across, riem, cluster, slot_row,
        face_partner, relax_time.reshape(1, owned), yield_flag.reshape(1, owned),
        cost=pl.CostEstimate(flops=10**8, bytes_accessed=4 * 10**6, transcendentals=0),
        name="own",
    )

    return call(
        final_kernel, plan,
        shape((QUANT, MODES, LANES), f32),
        [
            pltpu.VMEM((plan.n_reg, VT, SUB, LANES), f32),
            pltpu.VMEM((4, 3 * MODES, QUANT * LANES), bf16),
            pltpu.VMEM((4 * MODES, QUANT * LANES), f32),
            pltpu.VMEM((4, QUANT, MT, SUB, LANES), f32),
        ],
        *gots, requests[1], partial, near, across, riem, face_partner, partner_face,
        cohesion.reshape(1, owned), gain, name="final",
    )


def solution(mesh):
    n_dom, n_grp = mesh.shape["dom"], mesh.shape["grp"]
    both = ("dom", "grp")
    in_specs = (
        P(None, None, both), P(), P(None, None, None, both), P(), P(),
        P(None, None, None, None, both), P(both), P(both), P(None, both), P(None, both),
        P(both), P(both), P(both),
    )

    def body(*args):
        return on_device(n_dom, n_grp, *args)

    return jax.shard_map(
        body, mesh=mesh, in_specs=in_specs, out_specs=P(None, None, both), check_vma=False
    )
```

time: 32.6 us -> 34.8 us (1.067)
  Pallas kernels: 13.5 us -> 16.6 us
  waiting for transfers between devices: 3.26 us -> 2.41 us
    pallas_call x5 -> x6, Pallas kernels: 13.5 us -> 16.6 us  [call(): pl.pallas_call(body, out_shape=out_shape, in_specs=spaces or [vmem] * len...]
    ppermute x9, waiting for transfers between devices: 3.26 us -> 2.41 us  [the longest x4 2.39 us: on_device(): wanted[k] = lax.ppermute(requests[k], *plan.route[k])]
    unnamed x28 -> x26, local copies, waits for them, and re-layouts: 5.09 us -> 4.77 us
  transfers between devices with their start and end apart: 9 -> 9, of which waited for: 2 -> 2; matrix products, arithmetic and copies ran while one was open for 0% -> 0% of each run, Pallas kernels for 22% -> 36%
where the time goes in v2:
time: 34.8 us; the launch traced here: 34.4 us
  Pallas kernels  16.6 us (48%)
  starting transfers between devices  10.5 us (30%)
  local copies, waits for them, and re-layouts  4.78 us (14%)
  waiting for transfers between devices  2.41 us (7%)
    pallas_call x6, Pallas kernels, call(): pl.pallas_call(body, out_shape=out_shape, in_specs=spaces or [vmem] * len...  16.6 us
    ppermute x5, starting transfers between devices, on_device(): gots[k] = lax.ppermute(message, *plan.route[k])  5.92 us
    unnamed x26, local copies, waits for them, and re-layouts  4.77 us
    ppermute x4, starting transfers between devices, on_device(): wanted[k] = lax.ppermute(requests[k], *plan.route[k])  4.55 us
    ppermute x4, waiting for transfers between devices, on_device(): wanted[k] = lax.ppermute(requests[k], *plan.route[k])  2.39 us
  transfers between devices with their start and end apart: 9, of which 2 were waited for; matrix products, arithmetic and copies ran while one was open for 0% of the time, Pallas kernels for 36%

profile of v2, /device:TPU:0, one launch (start us, length us, event | category | flops | bytes accessed | tf_op | source)
XLA Modules:
  0.0 34.4 jit_solution(8100001199268172922)
XLA Ops:
  0.0 0.0 copy-start.6
  0.0 0.0 copy-start.8
  0.0 0.7 %copy-done.6 = s32[4,128]{1,0:T(4,128)S(1)} copy-done((s32[4,128]{1,0:T(4,128)S(1)}, s32[4,128]{1,0:T(4,128)}, u32[]{:S(2)}) %copy-start.6) | copy-done | bytes 2072
  0.7 0.0 copy-done.8
  0.7 0.0 copy-start.2
  0.7 0.9 %copy-done.2 = f32[9,56,128]{2,1,0:T(8,128)S(1)} copy-done((f32[9,56,128]{2,1,0:T(8,128)S(1)}, f32[9,56,128]{2,1,0:T(8,128)}, u32[]{:S(2)}) %copy-start.2) | copy-done | bytes 258072
  1.6 0.0 copy-start.3
  1.6 0.9 %copy-done.3 = f32[3,9,9,128]{3,0,2,1:T(4,128)S(1)} copy-done((f32[3,9,9,128]{3,0,2,1:T(4,128)S(1)}, f32[3,9,9,128]{3,0,2,1:T(4,128)}, u32[]{:S(2)}) %copy-start.3) | copy-done | bytes 124440
  2.6 0.0 copy-start.5
  2.6 0.9 %copy-done.5 = f32[3,56,56]{2,1,0:T(8,128)S(1)} copy-done((f32[3,56,56]{2,1,0:T(8,128)S(1)}, f32[3,56,56]{2,1,0:T(8,128)}, u32[]{:S(2)}) %copy-start.5) | copy-done | bytes 37656
  3.4 0.8 %requests.1 = (s32[8,128]{1,0:T(8,128)S(1)}, s32[8,128]{1,0:T(8,128)S(1)}, s32[8,128]{1,0:T(8,128)S(1)}, s32[8,128]{1,0:T(8,128)S(1)}, s32[8,128]{1,0:T(8,128)S(...) custom-call(s32[4,128]{1,0:T(4,128)S(1)} %copy-done.6, ...), custom_call_target="tpu_custom_call" | custom-call | tf_op jit(solution)/shard_map/requests/pallas_call | solution.py:401
  4.2 0.0 copy-start.12
  4.2 3.1 %collective-permute-start = (s32[8,128]{1,0:T(8,128)S(1)}, s32[8,128]{1,0:T(8,128)S(1)}, u32[]{:S(2)}, u32[]{:S(2)}) collective-permute-start(s32[8,128]{1,0:T(8,128)S(1)} %get-tuple-element.25), channel_id=1, source_target_pairs={{0,4},{4,0},{8,12},{12,8},{16,20},{20,16},{24,28},{28,24},{1,5},{5... | collective-permute-start | bytes 12296 | tf_op jit(solution)/shard_map/ppermute | solution.py:443
  7.3 0.0 collective-permute-start.1
  7.3 0.0 copy-done.12
  7.3 6.1 %predictor.1.refs_0_ = f32[3,64,8,128]{3,2,1,0:T(8,128)S(1)} custom-call(f32[9,56,128]{2,1,0:T(8,128)S(1)} %get-tuple-element.22.refs_0_.refs_1_, f32[3,56,56]{2,1,0:T(8,128)S(1)} %get-tuple-element.23.refs_1_.refs_2_, f32[9,9,3,128]{3,2,1,0:T(4,128)S(1)} %get-tuple-element.24.refs_2_.refs_3_), custom_call_target="tpu_custom_call" | custom-call | tf_op jit(solution)/shard_map/predictor/pallas_call | solution.py:401
  13.4 0.0 collective-permute-done.refs_2_
  13.4 0.0 collective-permute-done.1.refs_3_
  13.4 0.0 copy-start.4
  13.4 0.6 %sends_0.1 = (f32[16,8,128]{2,1,0:T(8,128)S(1)}, f32[48,8,128]{2,1,0:T(8,128)S(1)}, f32[32,8,128]{2,1,0:T(8,128)S(1)}) custom-call(f32[3,64,8,128]{3,2,1,0:T(8,128)S(1)} %predictor.1.refs_0_, s32[1,320]{1,0:T(1,128)S(1)} %reshape.16.refs_1_.refs_8_, s32[8,128]{1,0:T(8,128)S(1)} %collective-permute-done.refs_2_, s32[8,128]{1,0:T(8,128)S(1)} %collective-permute-done.1.refs_3_), custom_call_target="tpu_custom_call" | custom-call | tf_op jit(solution)/shard_map/sends_0/pallas_call | solution.py:401
  14.0 0.0 copy-start.1
  14.0 3.7 %collective-permute-start.3 = (f32[48,8,128]{2,1,0:T(8,128)S(1)}, f32[48,8,128]{2,1,0:T(8,128)S(1)}, u32[]{:S(2)}, u32[]{:S(2)}) collective-permute-start(f32[48,8,128]{2,1,0:T(8,128)S(1)} %get-tuple-element.28), channel_id=1, source_target_pairs={{0,28},{4,8},{8,4},{12,16},{16,12},{20,24},{24,20},{28,0},{1,29},{... | collective-permute-start | bytes 589832 | tf_op jit(solution)/shard_map/ppermute | solution.py:468
  17.7 1.5 %collective-permute-start.5 = (s32[8,128]{1,0:T(8,128)S(1)}, s32[8,128]{1,0:T(8,128)S(1)}, u32[]{:S(2)}, u32[]{:S(2)}) collective-permute-start(s32[8,128]{1,0:T(8,128)S(1)} %get-tuple-element.30), channel_id=1, source_target_pairs={{0,2},{1,3},{2,0},{3,1},{4,6},{5,7},{6,4},{7,5},{8,10},{9,11},{10,... | collective-permute-start | bytes 12296 | tf_op jit(solution)/shard_map/ppermute | solution.py:443
  19.2 0.0 collective-permute-start.6
  19.2 0.0 copy-start
  19.2 0.6 %collective-permute-start.4 = (f32[32,8,128]{2,1,0:T(8,128)S(1)}, f32[32,8,128]{2,1,0:T(8,128)S(1)}, u32[]{:S(2)}, u32[]{:S(2)}) collective-permute-start(f32[32,8,128]{2,1,0:T(8,128)S(1)} %get-tuple-element.29), channel_id=1, source_target_pairs={{0,1},{1,0},{2,3},{3,2},{4,5},{5,4},{6,7},{7,6},{8,9},{9,8},{10,11... | collective-permute-start | bytes 393224 | tf_op jit(solution)/shard_map/ppermute | solution.py:468
  19.8 1.5 %collective-permute-done.5.refs_2_ = s32[8,128]{1,0:T(8,128)S(1)} collective-permute-done((s32[8,128]{1,0:T(8,128)S(1)}, s32[8,128]{1,0:T(8,128)S(1)}, u32[]{:S(2)}, u32[]{:S(2)}) %collective-permute-start.5) | collective-permute-done | bytes 4128 | tf_op jit(solution)/shard_map/ppermute | solution.py:443
  21.3 0.9 %collective-permute-done.6.refs_3_ = s32[8,128]{1,0:T(8,128)S(1)} collective-permute-done((s32[8,128]{1,0:T(8,128)S(1)}, s32[8,128]{1,0:T(8,128)S(1)}, u32[]{:S(2)}, u32[]{:S(2)}) %collective-permute-start.6) | collective-permute-done | bytes 4128 | tf_op jit(solution)/shard_map/ppermute | solution.py:443
  22.2 0.5 %sends_1.1 = (f32[32,8,128]{2,1,0:T(8,128)S(1)}, f32[32,8,128]{2,1,0:T(8,128)S(1)}) custom-call(f32[3,64,8,128]{3,2,1,0:T(8,128)S(1)} %predictor.1.refs_0_, s32[1,320]{1,0:T(1,128)S(1)} %reshape.16.refs_1_.refs_8_, s32[8,128]{1,0:T(8,128)S(1)} %collective-permute-done.5.refs_2_, s32[8,128]{1,0:T(8,128)S(1)} %collective-permute-done.6.refs_3_), custom_call_target="tpu_custom_call" | custom-call | tf_op jit(solution)/shard_map/sends_1/pallas_call | solution.py:401
  22.7 0.6 %collective-permute-start.7 = (f32[32,8,128]{2,1,0:T(8,128)S(1)}, f32[32,8,128]{2,1,0:T(8,128)S(1)}, u32[]{:S(2)}, u32[]{:S(2)}) collective-permute-start(f32[32,8,128]{2,1,0:T(8,128)S(1)} %get-tuple-element.32), channel_id=1, source_target_pairs={{0,2},{1,3},{2,0},{3,1},{4,6},{5,7},{6,4},{7,5},{8,10},{9,11},{10,... | collective-permute-start | bytes 393224 | tf_op jit(solution)/shard_map/ppermute | solution.py:468
  23.4 0.9 %collective-permute-start.8 = (f32[32,8,128]{2,1,0:T(8,128)S(1)}, f32[32,8,128]{2,1,0:T(8,128)S(1)}, u32[]{:S(2)}, u32[]{:S(2)}) collective-permute-start(f32[32,8,128]{2,1,0:T(8,128)S(1)} %get-tuple-element.33), channel_id=1, source_target_pairs={{0,3},{1,2},{2,1},{3,0},{4,7},{5,6},{6,5},{7,4},{8,11},{9,10},{10,... | collective-permute-start | bytes 393224 | tf_op jit(solution)/shard_map/ppermute | solution.py:468
  24.3 0.0 collective-permute-start.2
  24.3 0.0 copy-start.9
  24.3 0.0 copy-start.10
  24.3 0.0 copy-done.4
  24.3 0.0 copy-done.1
  24.3 0.0 copy-done
  24.3 0.6 %copy-done.9 = f32[128]{0:T(128)S(1)} copy-done((f32[128]{0:T(128)S(1)}, f32[128]{0:T(128)}, u32[]{:S(2)}) %copy-start.9) | copy-done | bytes 536
  25.0 0.0 copy-done.10
  25.0 5.9 %own.1 = (f32[63,8,128]{2,1,0:T(8,128)S(1)}, f32[4,63,8,128]{3,2,1,0:T(8,128)S(1)}, bf16[4,224,168]{2,1,0:T(8,128)(2,1)S(1)}, f32[8,128]{1,0:T(8,128)S(1)}) custom-call(f32[3,64,8,128]{3,2,1,0:T(8,128)S(1)} %predictor.1.refs_0_, f32[9,56,128]{2,1,0:T(8,128)S(1)} %get-tuple-element.22.refs_0_.refs_1_, f32[3,56,56]{2,1,0:T(8,128)S(1)} %get-tuple-element.23.refs_1_.refs_2_, ...), custom_call_target="tpu_custom_call" | custom-call | flops 100000000 | bytes 4000000 | tf_op jit(solution)/shard_map/own/pallas_call | solution.py:401
  30.8 0.0 collective-permute-done.2.refs_0_
  30.9 0.0 collective-permute-done.4.refs_2_
  30.9 0.0 collective-permute-done.7.refs_3_
  30.9 0.0 collective-permute-done.8.refs_4_
  30.9 0.0 collective-permute-done.3.refs_1_
  30.9 0.0 copy-start.7
  30.9 0.0 copy-start.11
  30.9 0.7 %copy-done.7 = s32[4,128]{1,0:T(4,128)S(1)} copy-done((s32[4,128]{1,0:T(4,128)S(1)}, s32[4,128]{1,0:T(4,128)}, u32[]{:S(2)}) %copy-start.7) | copy-done | bytes 2072
  31.6 0.0 copy-done.11
  31.6 2.8 %final.1 = f32[9,56,128]{2,1,0:T(8,128)} custom-call(f32[16,8,128]{2,1,0:T(8,128)S(1)} %collective-permute-done.2.refs_0_, f32[48,8,128]{2,1,0:T(8,128)S(1)} %collective-permute-done.3.refs_1_, f32[32,8,128]{2,1,0:T(8,128)S(1)} %collective-permute-done.4.refs_2_, f32[32,8,128]{2,1,0:T(8,128)S(1)} %collective-permute-done.7.refs_3_, ...), custom_call_target="tpu_custom_call" | custom-call | tf_op jit(solution)/shard_map/final/pallas_call | solution.py:401
  (1 shorter events, 0.0 us)
Async XLA Ops:
  0.0 0.7 %copy-start.6 = (s32[4,128]{1,0:T(4,128)S(1)}, s32[4,128]{1,0:T(4,128)}, u32[]{:S(2)}) copy-start(s32[4,128]{1,0:T(4,128)} %refs_10_.1) | copy-start | bytes 6148
  0.0 0.7 %copy-start.8 = (s32[128]{0:T(128)S(1)}, s32[128]{0:T(128)}, u32[]{:S(2)}) copy-start(s32[128]{0:T(128)} %param.19) | copy-start | bytes 1540
  0.7 0.9 %copy-start.2 = (f32[9,56,128]{2,1,0:T(8,128)S(1)}, f32[9,56,128]{2,1,0:T(8,128)}, u32[]{:S(2)}) copy-start(f32[9,56,128]{2,1,0:T(8,128)} %refs_2_.1) | copy-start | bytes 774148
  1.6 0.9 %copy-start.3 = (f32[3,9,9,128]{3,0,2,1:T(4,128)S(1)}, f32[3,9,9,128]{3,0,2,1:T(4,128)}, u32[]{:S(2)}) copy-start(f32[3,9,9,128]{3,0,2,1:T(4,128)} %param.15) | copy-start | bytes 373252
  2.6 0.9 %copy-start.5 = (f32[3,56,56]{2,1,0:T(8,128)S(1)}, f32[3,56,56]{2,1,0:T(8,128)}, u32[]{:S(2)}) copy-start(f32[3,56,56]{2,1,0:T(8,128)} %refs_3_.1) | copy-start | bytes 112900
  4.2 3.1 %copy-start.12 = (s32[320]{0:T(512)S(1)}, s32[320]{0:T(512)}, u32[]{:S(2)}) copy-start(s32[320]{0:T(512)} %param.20) | copy-start | bytes 3844
  4.2 9.1 %collective-permute-start = (s32[8,128]{1,0:T(8,128)S(1)}, s32[8,128]{1,0:T(8,128)S(1)}, u32[]{:S(2)}, u32[]{:S(2)}) collective-permute-start(s32[8,128]{1,0:T(8,128)S(1)} %get-tuple-element.25), channel_id=1, source_target_pairs={{0,4},{4,0},{8,12},{12,8},{16,20},{20,16},{24,28},{28,24},{1,5},{5... | collective-permute-start | bytes 12296 | tf_op jit(solution)/shard_map/ppermute | solution.py:443
  7.3 6.1 %collective-permute-start.1 = (s32[8,128]{1,0:T(8,128)S(1)}, s32[8,128]{1,0:T(8,128)S(1)}, u32[]{:S(2)}, u32[]{:S(2)}) collective-permute-start(s32[8,128]{1,0:T(8,128)S(1)} %get-tuple-element.26), channel_id=1, source_target_pairs={{0,1},{1,0},{2,3},{3,2},{4,5},{5,4},{6,7},{7,6},{8,9},{9,8},{10,11... | collective-permute-start | bytes 12296 | tf_op jit(solution)/shard_map/ppermute | solution.py:443
  13.4 10.9 %copy-start.4 = (f32[4,56,56]{2,1,0:T(8,128)S(1)}, f32[4,56,56]{2,1,0:T(8,128)}, u32[]{:S(2)}) copy-start(f32[4,56,56]{2,1,0:T(8,128)} %refs_4_.1) | copy-start | bytes 150532
  14.0 10.3 %copy-start.1 = (f32[4,4,56,56]{3,2,1,0:T(8,128)S(1)}, f32[4,4,56,56]{3,2,1,0:T(8,128)}, u32[]{:S(2)}) copy-start(f32[4,4,56,56]{3,2,1,0:T(8,128)} %refs_5_.1) | copy-start | bytes 602116
  14.0 16.9 %collective-permute-start.3 = (f32[48,8,128]{2,1,0:T(8,128)S(1)}, f32[48,8,128]{2,1,0:T(8,128)S(1)}, u32[]{:S(2)}, u32[]{:S(2)}) collective-permute-start(f32[48,8,128]{2,1,0:T(8,128)S(1)} %get-tuple-element.28), channel_id=1, source_target_pairs={{0,28},{4,8},{8,4},{12,16},{16,12},{20,24},{24,20},{28,0},{1,29},{... | collective-permute-start | bytes 589832 | tf_op jit(solution)/shard_map/ppermute | solution.py:468
  17.7 3.6 %collective-permute-start.5 = (s32[8,128]{1,0:T(8,128)S(1)}, s32[8,128]{1,0:T(8,128)S(1)}, u32[]{:S(2)}, u32[]{:S(2)}) collective-permute-start(s32[8,128]{1,0:T(8,128)S(1)} %get-tuple-element.30), channel_id=1, source_target_pairs={{0,2},{1,3},{2,0},{3,1},{4,6},{5,7},{6,4},{7,5},{8,10},{9,11},{10,... | collective-permute-start | bytes 12296 | tf_op jit(solution)/shard_map/ppermute | solution.py:443
  19.2 3.0 %collective-permute-start.6 = (s32[8,128]{1,0:T(8,128)S(1)}, s32[8,128]{1,0:T(8,128)S(1)}, u32[]{:S(2)}, u32[]{:S(2)}) collective-permute-start(s32[8,128]{1,0:T(8,128)S(1)} %get-tuple-element.31), channel_id=1, source_target_pairs={{0,3},{1,2},{2,1},{3,0},{4,7},{5,6},{6,5},{7,4},{8,11},{9,10},{10,... | collective-permute-start | bytes 12296 | tf_op jit(solution)/shard_map/ppermute | solution.py:443
  19.2 5.1 %copy-start = (f32[2,4,9,9,128]{4,1,3,2,0:T(4,128)S(1)}, f32[2,4,9,9,128]{4,1,3,2,0:T(4,128)}, u32[]{:S(2)}) copy-start(f32[2,4,9,9,128]{4,1,3,2,0:T(4,128)} %param.18) | copy-start | bytes 995332
  19.2 11.7 %collective-permute-start.4 = (f32[32,8,128]{2,1,0:T(8,128)S(1)}, f32[32,8,128]{2,1,0:T(8,128)S(1)}, u32[]{:S(2)}, u32[]{:S(2)}) collective-permute-start(f32[32,8,128]{2,1,0:T(8,128)S(1)} %get-tuple-element.29), channel_id=1, source_target_pairs={{0,1},{1,0},{2,3},{3,2},{4,5},{5,4},{6,7},{7,6},{8,9},{9,8},{10,11... | collective-permute-start | bytes 393224 | tf_op jit(solution)/shard_map/ppermute | solution.py:468
  22.7 8.1 %collective-permute-start.7 = (f32[32,8,128]{2,1,0:T(8,128)S(1)}, f32[32,8,128]{2,1,0:T(8,128)S(1)}, u32[]{:S(2)}, u32[]{:S(2)}) collective-permute-start(f32[32,8,128]{2,1,0:T(8,128)S(1)} %get-tuple-element.32), channel_id=1, source_target_pairs={{0,2},{1,3},{2,0},{3,1},{4,6},{5,7},{6,4},{7,5},{8,10},{9,11},{10,... | collective-permute-start | bytes 393224 | tf_op jit(solution)/shard_map/ppermute | solution.py:468
  23.4 7.5 %collective-permute-start.8 = (f32[32,8,128]{2,1,0:T(8,128)S(1)}, f32[32,8,128]{2,1,0:T(8,128)S(1)}, u32[]{:S(2)}, u32[]{:S(2)}) collective-permute-start(f32[32,8,128]{2,1,0:T(8,128)S(1)} %get-tuple-element.33), channel_id=1, source_target_pairs={{0,3},{1,2},{2,1},{3,0},{4,7},{5,6},{6,5},{7,4},{8,11},{9,10},{10,... | collective-permute-start | bytes 393224 | tf_op jit(solution)/shard_map/ppermute | solution.py:468
  24.3 6.5 %collective-permute-start.2 = (f32[16,8,128]{2,1,0:T(8,128)S(1)}, f32[16,8,128]{2,1,0:T(8,128)S(1)}, u32[]{:S(2)}, u32[]{:S(2)}) collective-permute-start(f32[16,8,128]{2,1,0:T(8,128)S(1)} %get-tuple-element.27), channel_id=1, source_target_pairs={{0,4},{4,0},{8,12},{12,8},{16,20},{20,16},{24,28},{28,24},{1,5},{5... | collective-permute-start | bytes 196616 | tf_op jit(solution)/shard_map/ppermute | solution.py:468
  24.3 0.7 %copy-start.9 = (f32[128]{0:T(128)S(1)}, f32[128]{0:T(128)}, u32[]{:S(2)}) copy-start(f32[128]{0:T(128)} %param.24) | copy-start | bytes 1540
  24.3 0.7 %copy-start.10 = (s32[128]{0:T(128)S(1)}, s32[128]{0:T(128)}, u32[]{:S(2)}) copy-start(s32[128]{0:T(128)} %param.25) | copy-start | bytes 1540
  30.9 0.7 %copy-start.7 = (s32[4,128]{1,0:T(4,128)S(1)}, s32[4,128]{1,0:T(4,128)}, u32[]{:S(2)}) copy-start(s32[4,128]{1,0:T(4,128)} %refs_11_.1) | copy-start | bytes 6148
  30.9 0.7 %copy-start.11 = (f32[128]{0:T(128)S(1)}, f32[128]{0:T(128)}, u32[]{:S(2)}) copy-start(f32[128]{0:T(128)} %param.23) | copy-start | bytes 1540
